TPU v7x, 32 devices: a whole 2x2x4 slice. The times are simulated.
32 devices in a mesh: groups: 2 (over x), blk: 16 (over z, y, core).
Axes of the slice: x: 2, y: 2, z: 4, core: 2. Of those that a mesh axis runs over, the one named last changes fastest.
Arguments:
- hidden: bfloat16 [16384, 2048], P(('groups', 'blk')), parts along dimension 0, may hold values from -6 to 6
- kept_idx: int32 [32, 128], P(('groups', 'blk')), parts along dimension 0, may hold values from 0 to 511, as said below
- kept_count: int32 [32], P(('groups', 'blk')), parts along dimension 0, may hold values from 0 to 128, as said below
- router: bfloat16 [2048], replicated, may hold values from -0.125 to 0.125
- norm_gain: float32 [2048], replicated, may hold values from 0.25 to 1.75
- qk_gain: float32 [2, 64], replicated, may hold values from 1 to 7
- query_weight: bfloat16 [2048, 2048], P('blk'), may hold values from -1 to 1
- key_weight: bfloat16 [2048, 128], P('blk'), may hold values from -1 to 1
- value_weight: bfloat16 [2048, 128], P('blk'), may hold values from -0.125 to 0.125
- out_weight: bfloat16 [2048, 2048], P('blk'), may hold values from -0.375 to 0.375
Outputs:
- mixed: bfloat16 [16384, 2048], P(('groups', 'blk')), parts along dimension 0
There are 2 independent parts, one for each index of `groups`. A program takes and returns all parts, laid end to end along the dimension named above; an argument that names none is the same for every part. Nothing has to cross between parts.
Inputs may be any that keep to these rules, and one draw needn't show every extreme that they name: `kept_count`: the counts sum to 1024; in every draw some shard's count is exactly 128. `kept_idx`: in row s the first kept_count[s] entries are distinct local token indices in increasing order; entries past the count are 0.
All inputs are finite; a program needn't handle non-finite values.
Results may differ from a plain program's by a relative error of at most 0.01.
Values may be sent and summed in bfloat16 or wider, within the bound.
A program may use at most 128 MiB of HBM per device.

v0:
```python
import functools
import math

import jax
import jax.numpy as jnp
import numpy as np
from jax import lax
from jax.experimental import pallas as pl
from jax.experimental.pallas import tpu as pltpu
from jax.sharding import PartitionSpec as P

Q_HEADS = 32
KV_HEADS = 2
HEAD = 64
TOK_DEV = 512
KEEP_DEV = 64
CAP = 128
MESH = pl.DeviceIdType.MESH
VM = pl.BlockSpec(memory_space=pltpu.VMEM)


norm_eps = 1e-06
rope_base = 1000000.0


def rms_scale(values, scales):
    return values * lax.rsqrt(jnp.mean(values * values, axis=-1, keepdims=True) + norm_eps) * scales


def rotate(values, angles):
    half_size = values.shape[-1] // 2
    lower_half = values[..., :half_size]
    upper_half = values[..., half_size:]
    cosine = jnp.cos(angles)
    sine_part = jnp.sin(angles)
    return jnp.concatenate(
        [
            lower_half * cosine - upper_half * sine_part,
            upper_half * cosine + lower_half * sine_part,
        ],
        axis=-1,
    )


class Ring:
    def __init__(self, n):
        self.chips = n // 2
        self.arm = self.chips // 2
        self.me = lax.axis_index("blk")
        self.chip, self.core = self.me // 2, self.me % 2
        side, row = self.chip % 2, self.chip // 2
        self.place = row * (1 - side) + (self.chips - 1 - row) * side
        self.partner = self.chip * 2 + 1 - self.core
        self.ahead = self.device(self.place + 1, self.core)
        self.behind = self.device(self.place - 1, self.core)

    def device(self, position, on_core):
        q = lax.rem(position + 2 * self.chips, self.chips)
        far = q // self.arm
        chip_id = 2 * (q * (1 - far) + (self.chips - 1 - q) * far) + far
        return chip_id * 2 + on_core

    def target(self, step, u):
        return self.place - 1 - step if u % 2 == 0 else self.place + 1 + step


class RingSum:
    def __init__(self, ring, chunk, units, bufs, finish):
        self.ring, self.chunk, self.units, self.bufs, self.finish = ring, chunk, units, bufs, finish

    @staticmethod
    def scratch(chips, u, r, c):
        return [
            pltpu.VMEM((chips, u, r, c), jnp.bfloat16),
            pltpu.VMEM((chips, u, r, c), jnp.bfloat16),
            pltpu.VMEM((chips - 1, u, r, c), jnp.bfloat16),
            pltpu.VMEM((chips - 1, u, r, c), jnp.bfloat16),
            pltpu.SemaphoreType.DMA((chips, u)),
            pltpu.SemaphoreType.DMA((chips, u)),
            pltpu.SemaphoreType.DMA((chips - 1, u)),
            pltpu.SemaphoreType.DMA((chips - 1, u)),
        ]

    def copy(self, pair, step, u):
        pair_out, pair_in, ring_out, ring_in, ps, pr, rs, rr = self.bufs
        src, dst, ss, sr = (pair_out, pair_in, ps, pr) if pair else (ring_out, ring_in, rs, rr)
        to = self.ring.partner if pair else (self.ring.ahead if u % 2 == 0 else self.ring.behind)
        return pltpu.make_async_remote_copy(
            src_ref=src.at[step, u],
            dst_ref=dst.at[step, u],
            send_sem=ss.at[step, u],
            recv_sem=sr.at[step, u],
            device_id={"blk": to},
            device_id_type=MESH,
        )

    def pair_send(self, step):
        ring = self.ring
        for u in range(self.units):
            dest = ring.device(ring.target(step, u), 1 - ring.core)
            self.bufs[0][step, u] = self.chunk(dest, u).astype(jnp.bfloat16)
            self.copy(True, step, u).start()

    def advance(self, step):
        ring = self.ring
        for u in range(self.units):
            total = self.chunk(ring.device(ring.target(step, u), ring.core), u)
            self.copy(True, step, u).wait_recv()
            total = total + self.bufs[1][step, u].astype(jnp.float32)
            if step > 0:
                self.copy(False, step - 1, u).wait_recv()
                total = total + self.bufs[3][step - 1, u].astype(jnp.float32)
            if step + 1 < ring.chips:
                self.bufs[2][step, u] = total.astype(jnp.bfloat16)
                self.copy(False, step, u).start()
            else:
                self.finish(u, total)

    def drain(self):
        for step in range(self.ring.chips):
            for u in range(self.units):
                self.copy(True, step, u).wait_send()
                if step + 1 < self.ring.chips:
                    self.copy(False, step, u).wait_send()


def turn(values, cosine, sine, lane):
    swapped = jnp.where(lane % HEAD < HEAD // 2, pltpu.roll(values, 2 * HEAD - HEAD // 2, 1), pltpu.roll(values, HEAD // 2, 1))
    return values * cosine + swapped * sine


def layer_kernel(n, q_units, hidden_ref, idx_ref, count_ref, norm_ref, router_ref, wq_ref, wk_ref, wv_ref,
                 wo_ref, gain_ref, rate_ref, final_ref, normed_buf, meta_buf, x_ref, metas_ref, ranks_buf, rows_sum,
                 x_buf, pos_buf, kvp_buf, kv_lin, own_kv, all_kv, q_buf, att_buf, cos_buf, sin_buf,
                 strided_buf, product_buf, sum_buf, back_out, back_in,
                 spread_send, spread_recv, kv_send, kv_recv, back_send, back_recv, *bufs):
    ring = Ring(n)
    me, chips = ring.me, ring.chips
    barrier = pltpu.get_barrier_semaphore()
    for o in range(1, n):
        pl.semaphore_signal(
            barrier, inc=1, device_id={"blk": lax.rem(me + o, n)}, device_id_type=MESH
        )
    tokens = hidden_ref.shape[0]
    part, cap = x_ref.shape[-1], x_ref.shape[1]
    keep = x_buf.shape[0]
    own = keep // n
    lanes = 2 * HEAD
    q_rows, kv_rows = keep // q_units, own // 2

    pick = lax.broadcasted_iota(jnp.int32, (tokens, cap), 0) == idx_ref[...]
    token_rows = lax.dot_general(
        pick.astype(jnp.float32).astype(jnp.bfloat16),
        hidden_ref[...],
        (((0,), (0,)), ((), ())),
        preferred_element_type=jnp.float32,
    )
    final_ref[...] = token_rows.astype(jnp.bfloat16)
    normed_buf[...] = rms_scale(token_rows, norm_ref[...]).astype(jnp.bfloat16)
    line = lax.broadcasted_iota(jnp.int32, meta_buf.shape, 0)
    meta_buf[...] = jnp.where(line == 0, idx_ref[...], count_ref[...])

    def meta_copy(o, dest, place):
        return pltpu.make_async_remote_copy(
            src_ref=meta_buf,
            dst_ref=metas_ref.at[place],
            send_sem=spread_send.at[0, o],
            recv_sem=spread_recv.at[0, o],
            device_id={"blk": dest},
            device_id_type=MESH,
        )

    def rows_copy(o, dest, place):
        return pltpu.make_async_remote_copy(
            src_ref=normed_buf.at[:, pl.ds(pl.multiple_of(dest * part, part), part)],
            dst_ref=x_ref.at[place],
            send_sem=spread_send.at[1, o],
            recv_sem=spread_recv.at[1, o],
            device_id={"blk": dest},
            device_id_type=MESH,
        )

    pl.semaphore_wait(barrier, n - 1)
    for o in range(1, n):
        meta_copy(o, lax.rem(me + o, n), me).start()
    for o in range(1, n):
        rows_copy(o, lax.rem(me + o, n), me).start()
    x_ref[me] = normed_buf[:, pl.ds(pl.multiple_of(me * part, part), part)]
    metas_ref[me] = meta_buf[...]
    for o in range(1, n):
        source = lax.rem(me + n - o, n)
        meta_copy(o, source, source).wait_recv()

    starts, counts = [], []
    start = jnp.zeros((1, cap), jnp.int32)
    slot = lax.broadcasted_iota(jnp.int32, (1, cap), 1)
    block = 256
    for s in range(n):
        count = metas_ref[s, 1:2, :]
        starts.append(start)
        counts.append(count)
        ranks_buf[s, 0:1, :] = jnp.where(slot < count, start + slot, keep)
        start = start + count
    for o in range(n):
        source = lax.rem(me + n - o, n)
        if o > 0:
            rows_copy(o, source, source).wait_recv()
        place_row = (metas_ref[source, 0:1, :] + source * tokens).astype(jnp.float32)
        rank_row = ranks_buf[source, 0:1, :]
        found = x_ref[source]
        for b in range(keep // block):
            at = slice(b * block, (b + 1) * block)
            hit = lax.broadcasted_iota(jnp.int32, (block, cap), 0) + b * block == rank_row
            rows = jnp.dot(hit.astype(jnp.float32).astype(jnp.bfloat16), found, preferred_element_type=jnp.float32)
            spot = jnp.where(hit, place_row, 0.0)
            if o > 0:
                rows, spot = rows + rows_sum[at, :], spot + pos_buf[at, :]
            if o + 1 < n:
                rows_sum[at, :] = rows
                pos_buf[at, :] = spot
            else:
                x_buf[at, :] = rows.astype(jnp.bfloat16)
                pos_buf[at, :] = jnp.broadcast_to(jnp.sum(spot, axis=1, keepdims=True), (block, lanes))
    for g in range(KV_HEADS):
        weight = jnp.concatenate(
            [wk_ref[:, g * HEAD : (g + 1) * HEAD], wv_ref[:, g * HEAD : (g + 1) * HEAD]], axis=1
        )
        kvp_buf[:, g * lanes : (g + 1) * lanes] = jnp.dot(
            x_buf[...], weight, preferred_element_type=jnp.float32
        )

    def query_chunk(dest, u):
        cols = pl.ds(pl.multiple_of(dest * lanes, lanes), lanes)
        return jnp.dot(
            x_buf[u * q_rows : (u + 1) * q_rows, :], wq_ref[:, cols], preferred_element_type=jnp.float32
        )

    def kv_chunk(dest, u):
        return kvp_buf[pl.ds(pl.multiple_of(dest * own + u * kv_rows, kv_rows), kv_rows), :]

    def kv_finish(u, total):
        kv_lin[u * kv_rows : (u + 1) * kv_rows, :] = total

    lane = lax.broadcasted_iota(jnp.int32, (1, lanes), 1)
    sign = jnp.where(lane % HEAD < HEAD // 2, -1.0, 1.0)

    def query_finish(u, total):
        gain = jnp.concatenate([gain_ref[0:1, :], gain_ref[0:1, :]], axis=1)
        squares = total * total
        first = jnp.sum(jnp.where(lane < HEAD, squares, 0.0), axis=1, keepdims=True)
        second = jnp.sum(jnp.where(lane < HEAD, 0.0, squares), axis=1, keepdims=True)
        mean = jnp.where(lane < HEAD, first, second) * (1.0 / HEAD)
        values = total * lax.rsqrt(mean + norm_eps) * gain
        at = slice(u * q_rows, (u + 1) * q_rows)
        q_buf[at, :] = turn(values, cos_buf[at, :], sin_buf[at, :], lane).astype(jnp.bfloat16)

    kv_ring = RingSum(ring, kv_chunk, 2, bufs[:8], kv_finish)
    q_ring = RingSum(ring, query_chunk, q_units, bufs[8:16], query_finish)

    def kv_copy(o, dest, place):
        return pltpu.make_async_remote_copy(
            src_ref=own_kv.at[dest * KV_HEADS // n],
            dst_ref=all_kv.at[place],
            send_sem=kv_send.at[o],
            recv_sem=kv_recv.at[o],
            device_id={"blk": dest},
            device_id_type=MESH,
        )

    def share():
        angle = pos_buf[pl.ds(pl.multiple_of(me * own, own), own), :] * rate_ref[...]
        cosine, sine = jnp.cos(angle), jnp.sin(angle) * sign
        gain = jnp.concatenate([gain_ref[1:2, :], gain_ref[1:2, :]], axis=1)
        for g in range(KV_HEADS):
            both = kv_lin[:, g * lanes : (g + 1) * lanes]
            mean = jnp.sum(jnp.where(lane < HEAD, both * both, 0.0), axis=1, keepdims=True) * (1.0 / HEAD)
            key = turn(both * lax.rsqrt(mean + norm_eps) * gain, cosine, sine, lane)
            own_kv[g] = jnp.where(lane < HEAD, key, both).astype(jnp.bfloat16)
        for o in range(1, n):
            kv_copy(o, lax.rem(me + o, n), me).start()
        all_kv[me] = own_kv[me * KV_HEADS // n]

    kv_ring.pair_send(0)
    kv_ring.pair_send(1)
    q_ring.pair_send(0)
    table = keep // chips
    for step in range(chips):
        for k in (2 * step, 2 * step + 1):
            if k < chips:
                kv_ring.advance(k)
                if k + 2 < chips:
                    kv_ring.pair_send(k + 2)
                if k + 1 == chips:
                    share()
        if step + 1 < chips:
            q_ring.pair_send(step + 1)
        rows = slice(step * table, (step + 1) * table)
        angle = pos_buf[rows, :] * rate_ref[...]
        cos_buf[rows, :] = jnp.cos(angle)
        sin_buf[rows, :] = jnp.sin(angle) * sign
        q_ring.advance(step)
    for o in range(1, n):
        source = lax.rem(me + n - o, n)
        kv_copy(o, source, source).wait_recv()

    for begin in range(0, keep, block):
        end = begin + block
        pairs = all_kv[: end // own].reshape(end, lanes)
        row = lax.broadcasted_iota(jnp.int32, (block, end), 0) + begin
        col = lax.broadcasted_iota(jnp.int32, (block, end), 1)
        both = q_buf[begin:end, :].astype(jnp.float32)
        mixes = []
        for h in range(2):
            query = jnp.where(lane < HEAD, both if h == 0 else pltpu.roll(both, HEAD, 1), 0.0)
            scores = lax.dot_general(
                query.astype(jnp.bfloat16), pairs, (((1,), (1,)), ((), ())), preferred_element_type=jnp.float32
            ) * (1.0 / math.sqrt(HEAD))
            scores = jnp.where(col <= row, scores, -1e30)
            top = jnp.max(scores, axis=-1, keepdims=True)
            weights = jnp.exp(scores - top)
            denominator = jnp.sum(weights, axis=-1, keepdims=True)
            mix = jnp.dot(weights.astype(jnp.bfloat16), pairs, preferred_element_type=jnp.float32)
            mixes.append(mix / denominator)
        att_buf[begin:end, :] = jnp.where(lane < HEAD, pltpu.roll(mixes[0], HEAD, 1), mixes[1])

    for d in range(n):
        strided_buf[d * own : (d + 1) * own, :] = att_buf[pl.ds(d, own, stride=n), :].astype(jnp.bfloat16)
    for begin in range(0, keep, block):
        product_buf[begin : begin + block, :] = jnp.dot(
            strided_buf[begin : begin + block, :], wo_ref[...], preferred_element_type=jnp.float32
        )
    out_units = 4
    out_rows = own // out_units

    def out_chunk(dest, u):
        return product_buf[pl.ds(pl.multiple_of(dest * own + u * out_rows, out_rows), out_rows), :]

    def out_finish(u, total):
        sum_buf[u * out_rows : (u + 1) * out_rows, :] = total.astype(jnp.bfloat16)

    out_ring = RingSum(ring, out_chunk, out_units, bufs[16:], out_finish)
    out_ring.pair_send(0)
    for step in range(chips):
        if step + 1 < chips:
            out_ring.pair_send(step + 1)
        out_ring.advance(step)

    turns = cap // n
    hits = []
    k_iota = lax.broadcasted_iota(jnp.int32, (turns, own), 1)
    j_iota = lax.broadcasted_iota(jnp.int32, (turns, own), 0)
    start_own = jnp.zeros((1, cap), jnp.int32)
    for s in range(n):
        shift = lax.rem(me - starts[s] + keep, n)
        first = lax.div(starts[s] + shift - me, n)
        hits.append((k_iota - j_iota == first[:, :1]).astype(jnp.float32))
        start_own = start_own + jnp.where(me > s, counts[s], 0)
    back = jnp.dot(
        jnp.concatenate(hits, axis=0).astype(jnp.bfloat16), sum_buf[...], preferred_element_type=jnp.float32
    )
    for s in range(n):
        back_out[s] = back[s * turns : (s + 1) * turns, :].astype(jnp.bfloat16)

    def back_copy(o, dest, place):
        return pltpu.make_async_remote_copy(
            src_ref=back_out.at[dest],
            dst_ref=back_in.at[place],
            send_sem=back_send.at[o],
            recv_sem=back_recv.at[o],
            device_id={"blk": dest},
            device_id_type=MESH,
        )

    for o in range(1, n):
        back_copy(o, lax.rem(me + o, n), me).start()
    back_in[me] = back_out[me]
    rows = final_ref[...].astype(jnp.float32)
    gate = jax.nn.sigmoid(jnp.sum(rows * router_ref[...].astype(jnp.float32), axis=1, keepdims=True))
    column = lax.broadcasted_iota(jnp.int32, (1, cap), 1)
    slot_of = lax.rem(column, turns) * n + lax.rem(lax.div(column, turns) - start_own + keep, n)
    order = (lax.broadcasted_iota(jnp.int32, (cap, cap), 0) == slot_of).astype(jnp.float32)
    for o in range(1, n):
        source = lax.rem(me + n - o, n)
        back_copy(o, source, source).wait_recv()
    returned = jnp.concatenate([back_in[d].astype(jnp.float32) for d in range(n)], axis=0)
    update = jnp.dot(
        order.astype(jnp.bfloat16), returned.astype(jnp.bfloat16), preferred_element_type=jnp.float32
    )
    final_ref[...] = (rows + gate * update).astype(jnp.bfloat16)

    kv_ring.drain()
    q_ring.drain()
    out_ring.drain()
    for o in range(1, n):
        dest = lax.rem(me + o, n)
        kv_copy(o, dest, me).wait_send()
        back_copy(o, dest, me).wait_send()
        meta_copy(o, dest, me).wait_send()
        rows_copy(o, dest, me).wait_send()


def layer(n, keep, hidden, kept_idx, kept_count, router, norm_gain, qk_gain, query_weight, key_weight,
          value_weight, out_weight):
    tokens, width = hidden.shape
    cap, part = kept_idx.shape[1], width // n
    lanes, own, chips, q_units = 2 * HEAD, keep // n, n // 2, 4
    half_size = HEAD // 2
    rates = rope_base ** (-(np.arange(half_size) * 2.0 / HEAD))
    rates = np.tile(rates, lanes // half_size)[None, :].astype(np.float32)
    return pl.pallas_call(
        functools.partial(layer_kernel, n, q_units),
        out_shape=jax.ShapeDtypeStruct((cap, width), jnp.bfloat16),
        in_specs=[VM] * 11,
        out_specs=VM,
        scratch_shapes=[
            pltpu.VMEM((cap, width), jnp.bfloat16),
            pltpu.VMEM((8, cap), jnp.int32),
            pltpu.VMEM((n, cap, part), jnp.bfloat16),
            pltpu.VMEM((n, 8, cap), jnp.int32),
            pltpu.VMEM((n, 8, cap), jnp.int32),
            pltpu.VMEM((keep, part), jnp.float32),
            pltpu.VMEM((keep, part), jnp.bfloat16),
            pltpu.VMEM((keep, lanes), jnp.float32),
            pltpu.VMEM((keep, KV_HEADS * lanes), jnp.float32),
            pltpu.VMEM((own, KV_HEADS * lanes), jnp.float32),
            pltpu.VMEM((KV_HEADS, own, lanes), jnp.bfloat16),
            pltpu.VMEM((n, own, lanes), jnp.bfloat16),
            pltpu.VMEM((keep, lanes), jnp.bfloat16),
            pltpu.VMEM((keep, lanes), jnp.float32),
            pltpu.VMEM((keep, lanes), jnp.float32),
            pltpu.VMEM((keep, lanes), jnp.float32),
            pltpu.VMEM((keep, lanes), jnp.bfloat16),
            pltpu.VMEM((keep, width), jnp.float32),
            pltpu.VMEM((own, width), jnp.bfloat16),
            pltpu.VMEM((n, cap // n, width), jnp.bfloat16),
            pltpu.VMEM((n, cap // n, width), jnp.bfloat16),
            pltpu.SemaphoreType.DMA((2, n)),
            pltpu.SemaphoreType.DMA((2, n)),
            pltpu.SemaphoreType.DMA((n,)),
            pltpu.SemaphoreType.DMA((n,)),
            pltpu.SemaphoreType.DMA((n,)),
            pltpu.SemaphoreType.DMA((n,)),
        ]
        + RingSum.scratch(chips, 2, own // 2, KV_HEADS * lanes)
        + RingSum.scratch(chips, q_units, keep // q_units, lanes)
        + RingSum.scratch(chips, 4, own // 4, width),
        compiler_params=pltpu.CompilerParams(collective_id=1, has_side_effects=True),
    )(
        hidden, kept_idx, kept_count.reshape(1, 1), norm_gain.reshape(1, width), router.reshape(1, width),
        query_weight, key_weight, value_weight, out_weight, qk_gain, rates,
    )


def body(
    n,
    hidden,
    kept_idx,
    kept_count,
    router,
    norm_gain,
    qk_gain,
    query_weight,
    key_weight,
    value_weight,
    out_weight,
):
    tokens = hidden.shape[0]
    cap = kept_idx.shape[1]
    keep = n * (tokens * KEEP_DEV // TOK_DEV)
    final = layer(
        n, keep, hidden, kept_idx, kept_count, router, norm_gain, qk_gain, query_weight, key_weight,
        value_weight, out_weight,
    )
    slots = jnp.arange(cap, dtype=jnp.int32)
    put = (kept_idx == jnp.arange(tokens, dtype=jnp.int32)[:, None]) & (slots[None, :] < kept_count[0])
    placed = jnp.dot(put.astype(jnp.bfloat16), final, preferred_element_type=jnp.float32)
    return jnp.where(jnp.any(put, axis=1)[:, None], placed.astype(jnp.bfloat16), hidden)


def attend(query_heads, query_ranks, key_block, value_block, key_ranks, state):
    prev_top, prev_total, prev_acc = state
    length = key_block.shape[0]
    keys_split = key_block.reshape(length, KV_HEADS, HEAD)
    values_split = value_block.reshape(length, KV_HEADS, HEAD)
    scores = jnp.einsum(
        "agch,bgh->gcab", query_heads, keys_split, preferred_element_type=jnp.float32
    ) * (1.0 / math.sqrt(HEAD))
    allowed = key_ranks[None, :] <= query_ranks[:, None]
    masked = jnp.where(allowed, scores, -1e30)
    new_top = jnp.maximum(prev_top, jnp.max(masked, axis=-1))
    weights = jnp.where(allowed, jnp.exp(masked - new_top[..., None]), 0.0)
    factor = jnp.exp(prev_top - new_top)
    new_total = prev_total * factor + jnp.sum(weights, axis=-1)
    new_acc = prev_acc * factor[..., None] + jnp.einsum(
        "gcab,bgh->gcah",
        weights.astype(jnp.bfloat16),
        values_split,
        preferred_element_type=jnp.float32,
    )
    return (new_top, new_total, new_acc)


def make_fold(query_heads, query_ranks, rank_of, state, pieces):
    key_piece, value_piece = pieces
    length = key_piece.shape[0]

    def inner(block_turn, inner_state):
        block_start = block_turn * 512
        key_block = lax.dynamic_slice_in_dim(key_piece, block_start, 512, 0)
        value_block = lax.dynamic_slice_in_dim(value_piece, block_start, 512, 0)
        key_ranks = rank_of(block_start + jnp.arange(512, dtype=jnp.int32))
        return attend(query_heads, query_ranks, key_block, value_block, key_ranks, inner_state)

    return lax.fori_loop(0, length // 512, inner, state)


def wide_body(
    hidden,
    kept_idx,
    kept_count,
    router,
    norm_gain,
    qk_gain,
    query_weight,
    key_weight,
    value_weight,
    out_weight,
):
    shard_count = lax.axis_size("blk")
    device = lax.axis_index("blk")
    width = hidden.shape[1]
    all_lists, all_counts = (
        lax.all_gather(kept_idx, "blk", axis=0, tiled=True),
        lax.all_gather(kept_count, "blk", axis=0, tiled=True),
    )
    starts = jnp.cumsum(all_counts) - all_counts
    own_start = starts[device]
    own_count = all_counts[device]
    list_slots = jnp.arange(CAP, dtype=jnp.int32)
    is_valid = list_slots < own_count
    token_rows = hidden[kept_idx[0]]
    gate_value = jax.nn.sigmoid(jnp.dot(token_rows, router, preferred_element_type=jnp.float32))
    slot_count = (CAP + shard_count - 1) // shard_count
    outgoing = jnp.where(is_valid[:, None], token_rows, jnp.zeros_like(token_rows))
    outgoing = jnp.roll(outgoing.reshape(slot_count, shard_count, width), own_start, axis=1)
    incoming = lax.all_to_all(outgoing, "blk", split_axis=1, concat_axis=1, tiled=True)
    query_ranks = device + jnp.arange(KEEP_DEV, dtype=jnp.int32) * shard_count
    source_ends = starts + all_counts
    source = jnp.sum((source_ends[None, :] <= query_ranks[:, None]).astype(jnp.int32), axis=1)
    within = query_ranks - starts[source]
    flat_index = within // shard_count * shard_count + source
    kept_rows = incoming.reshape(slot_count * shard_count, width)[flat_index]
    positions = source * TOK_DEV + all_lists[source, within]
    row_total = kept_rows.shape[0]
    normed = rms_scale(kept_rows.astype(jnp.float32), norm_gain).astype(jnp.bfloat16)
    query_cols = Q_HEADS * HEAD
    kv_cols = KV_HEADS * HEAD
    full_query, full_key, full_value, full_out = (
        lax.all_gather(query_weight, "blk", axis=0, tiled=True),
        lax.all_gather(key_weight, "blk", axis=0, tiled=True),
        lax.all_gather(value_weight, "blk", axis=0, tiled=True),
        lax.all_gather(out_weight, "blk", axis=0, tiled=True),
    )
    query_lin = jnp.dot(normed, full_query, preferred_element_type=jnp.float32)
    key_lin = jnp.dot(normed, full_key, preferred_element_type=jnp.float32)
    value_lin = jnp.dot(normed, full_value, preferred_element_type=jnp.float32)
    half_size = HEAD // 2
    rotation_rates = rope_base ** (-(jnp.arange(half_size, dtype=jnp.float32) * 2.0 / HEAD))
    angles = (positions.astype(jnp.float32)[:, None] * rotation_rates[None, :])[:, None, :]
    query_heads = rotate(
        rms_scale(query_lin.reshape(row_total, Q_HEADS, HEAD), qk_gain[0]), angles
    ).astype(jnp.bfloat16)
    key_heads = rotate(
        rms_scale(key_lin.reshape(row_total, KV_HEADS, HEAD), qk_gain[1]), angles
    ).astype(jnp.bfloat16)
    query_heads = query_heads.reshape(row_total, KV_HEADS, Q_HEADS // KV_HEADS, HEAD)
    key_flat = key_heads.reshape(row_total, kv_cols)
    value_flat = value_lin.astype(jnp.bfloat16)
    group_size = Q_HEADS // KV_HEADS
    start_state = (
        jnp.full((KV_HEADS, group_size, row_total), -1e30, jnp.float32),
        jnp.zeros((KV_HEADS, group_size, row_total), jnp.float32),
        jnp.zeros((KV_HEADS, group_size, row_total, HEAD), jnp.float32),
    )

    def strided_rank(slots_seen):
        return slots_seen // KEEP_DEV + slots_seen % KEEP_DEV * shard_count

    final_top, final_total, final_acc = make_fold(
        query_heads,
        query_ranks,
        strided_rank,
        start_state,
        (
            lax.all_gather(key_flat, "blk", axis=0, tiled=True),
            lax.all_gather(value_flat, "blk", axis=0, tiled=True),
        ),
    )
    attended = (
        (final_acc / final_total[..., None])
        .transpose(2, 0, 1, 3)
        .reshape(row_total, query_cols)
        .astype(jnp.bfloat16)
    )
    update = jnp.dot(attended, full_out, preferred_element_type=jnp.float32)
    update = update.astype(jnp.bfloat16)
    slot_grid = (
        jnp.arange(slot_count, dtype=jnp.int32)[:, None] * shard_count
        + jnp.mod(device - starts, shard_count)[None, :]
    )
    back_valid = slot_grid < all_counts[None, :]
    local_place = (starts[None, :] + slot_grid - device) // shard_count
    clipped = jnp.where(back_valid, local_place, 0)
    back_rows = jnp.where(back_valid[..., None], update[clipped], jnp.zeros((), jnp.bfloat16))
    returned = lax.all_to_all(back_rows, "blk", split_axis=1, concat_axis=1, tiled=True)
    returned = jnp.roll(returned, -own_start, axis=1).reshape(slot_count * shard_count, width)
    final = (
        token_rows.astype(jnp.float32) + gate_value[:, None] * returned.astype(jnp.float32)
    ).astype(jnp.bfloat16)
    target = jnp.where(is_valid, kept_idx[0], TOK_DEV)
    return hidden.at[target].set(final, mode="drop")


def solution(mesh):
    placed = (
        P(("groups", "blk"), None),
        P(("groups", "blk"), None),
        P(("groups", "blk")),
        P(),
        P(),
        P(),
        P("blk", None),
        P("blk", None),
        P("blk", None),
        P("blk", None),
    )
    n = mesh.shape["blk"]
    by_heads = n % 4 == 0 and Q_HEADS == 2 * n
    step = functools.partial(body, n) if by_heads else wide_body
    return jax.shard_map(
        step, mesh=mesh, in_specs=placed, out_specs=P(("groups", "blk"), None), check_vma=False
    )
```

profile of v0, /device:TPU:1, one launch (start us, length us, event | category | flops | bytes accessed | tf_op | source)
XLA Modules:
  0.0 116.2 jit_solution(1275152674244494621)
XLA Ops:
  0.0 0.0 copy-start.1
  0.0 0.0 copy-start
  0.8 0.8 fusion.3
  1.6 1.3 %reshape.17.router_ref = bf16[1,2048]{1,0:T(2,128)(2,1)} reshape(bf16[2048]{0:T(1024)(128)(2,1)} %param.14) | data formatting | bytes 8192 | tf_op jit(solution)/shard_map/reshape | solution.py:449
  2.9 110.2 %shard_map.109 = bf16[128,2048]{1,0:T(8,128)(2,1)} custom-call(bf16[512,2048]{1,0:T(8,128)(2,1)} %hidden_ref.1, s32[1,128]{1,0:T(1,128)} %idx_ref.1, s32[1,1]{1,0:T(1,128)} %bitcast.6.count_ref, f32[1,2048]{1,0:T(1,128)} %bitcast.7, bf16[1,2048]{1,0:T(2,128)(2,1)} %reshape.17.router_ref, bf16[128,2048]{1,0:T(8,128)(2,1)} %wq_ref.1, bf16[128,128]{1,0:T(8,128)(2,1)} %wk_ref.1, ...), custom_call_target="tpu_custom_call" | custom-call | tf_op jit(solution)/shard_map/pallas_call | solution.py:410
  113.1 0.0 copy-done.1
  113.1 0.0 copy-done
  113.1 3.1 %fusion = bf16[512,2048]{1,0:T(8,128)(2,1)} fusion(bf16[512,2048]{1,0:T(8,128)(2,1)S(1)} %copy-done, bf16[128,2048]{1,0:T(8,128)(2,1)} %shard_map.109, pred[512]{0:T(512)(128)(4,1)S(1)} %fusion.3, s32[128]{0:T(128)S(1)} %bitcast.9, pred[128]{0:T(512)(128)(4,1)S(1)} %iota_compare_fusion.1), kind=kOutput, calls=%fused_computation.1 | convolution fusion | flops 270663680 | bytes 4719744 | tf_op jit(solution)/shard_map/dot_general | solution.py:476
  (1 shorter events, 0.0 us)
Async XLA Ops:
  0.0 113.1 %copy-start.1 = (s32[1,128]{1,0:T(1,128)S(1)}, s32[1,128]{1,0:T(1,128)}, u32[]{:S(2)}) copy-start(s32[1,128]{1,0:T(1,128)} %idx_ref.1) | copy-start | bytes 1540
  0.0 113.1 %copy-start = (bf16[512,2048]{1,0:T(8,128)(2,1)S(1)}, bf16[512,2048]{1,0:T(8,128)(2,1)}, u32[]{:S(2)}) copy-start(bf16[512,2048]{1,0:T(8,128)(2,1)} %hidden_ref.1) | copy-start | bytes 6291460
where the time goes:
time: 117 us; the launch traced here: 116 us
  Pallas kernels  110 us (94%)
  matrix products  3.07 us (3%)
  local copies, waits for them, and re-layouts  1.31 us (1%)
    pallas_call x1, Pallas kernels, layer(): pl.pallas_call(functools.partial(layer_kernel, n, q_units), out_shape=jax...  110 us
    dot_general x1, matrix products, body(): jnp.dot(put.astype(jnp.bfloat16), final, preferred_element_type=jnp.float32)  3.07 us

commit v1 on v0

v1 whole, which is shorter than its diff:
```python
import functools
import math

import jax
import jax.numpy as jnp
import numpy as np
from jax import lax
from jax.experimental import pallas as pl
from jax.experimental.pallas import tpu as pltpu
from jax.sharding import PartitionSpec as P

Q_HEADS = 32
KV_HEADS = 2
HEAD = 64
TOK_DEV = 512
KEEP_DEV = 64
CAP = 128
MESH = pl.DeviceIdType.MESH
VM = pl.BlockSpec(memory_space=pltpu.VMEM)


norm_eps = 1e-06
rope_base = 1000000.0


def rms_scale(values, scales):
    return values * lax.rsqrt(jnp.mean(values * values, axis=-1, keepdims=True) + norm_eps) * scales


def rotate(values, angles):
    half_size = values.shape[-1] // 2
    lower_half = values[..., :half_size]
    upper_half = values[..., half_size:]
    cosine = jnp.cos(angles)
    sine_part = jnp.sin(angles)
    return jnp.concatenate(
        [
            lower_half * cosine - upper_half * sine_part,
            upper_half * cosine + lower_half * sine_part,
        ],
        axis=-1,
    )


class Ring:
    def __init__(self, n):
        self.chips = n // 2
        self.arm = self.chips // 2
        self.me = lax.axis_index("blk")
        self.group = lax.axis_index("groups")
        self.chip, self.core = self.me // 2, self.me % 2
        side, row = self.chip % 2, self.chip // 2
        self.place = row * (1 - side) + (self.chips - 1 - row) * side
        self.partner = self.chip * 2 + 1 - self.core
        self.ahead = self.chip_at(self.place + 1) * 2 + self.core
        self.behind = self.chip_at(self.place - 1) * 2 + self.core

    def chip_at(self, position):
        q = lax.rem(position + 2 * self.chips, self.chips)
        far = q // self.arm
        return 2 * (q * (1 - far) + (self.chips - 1 - q) * far) + far


class Spread:
    def __init__(self, ring, own, buf, rows, sems, dup_sems=None, flip=False):
        self.ring, self.own, self.buf, self.rows, self.flip = ring, own, buf, rows, flip
        self.send, self.recv = sems
        self.dup_sems = dup_sems
        far = ring.chips // 2
        self.hops = {1: far - 1 if flip else far, -1: far if flip else far - 1}

    @staticmethod
    def semaphores(chips, count):
        return [pltpu.SemaphoreType.DMA((count, 2, chips // 2)) for _ in range(2)]

    def at(self, distance, sign, core):
        chip = self.ring.chip_at(self.ring.place - sign * distance)
        block = chip if self.dup_sems is None else chip * 2 + core
        return self.buf.at[pl.ds(pl.multiple_of(block * self.rows, self.rows), self.rows)]

    def copy(self, distance, sign, arriving):
        ring = self.ring
        place = self.at(distance if arriving else distance - 1, sign, ring.core)
        source = self.own if distance == 1 and not arriving else place
        k = 0 if sign > 0 else 1
        return pltpu.make_async_remote_copy(
            src_ref=source,
            dst_ref=place,
            send_sem=self.send.at[k, distance - 1],
            recv_sem=self.recv.at[k, distance - 1],
            device_id={"blk": ring.ahead if sign > 0 else ring.behind},
            device_id_type=MESH,
        )

    def dup(self, distance, sign, arriving=False):
        ring = self.ring
        core = 1 - ring.core if arriving else ring.core
        place = self.at(distance, sign, core)
        slot = distance if sign > 0 else self.hops[1] + distance
        source = self.own if distance == 0 and not arriving else place
        return pltpu.make_async_remote_copy(
            src_ref=source,
            dst_ref=place,
            send_sem=self.dup_sems[0].at[slot],
            recv_sem=self.dup_sems[1].at[slot],
            device_id={"blk": ring.partner},
            device_id_type=MESH,
        )

    def start(self):
        for sign in (1, -1):
            self.copy(1, sign, False).start()
        if self.dup_sems is not None:
            self.dup(0, 1).start()

    def serve(self, distance):
        for sign in (1, -1):
            if distance <= self.hops[sign]:
                self.copy(distance, sign, True).wait_recv()
                if distance < self.hops[sign]:
                    self.copy(distance + 1, sign, False).start()
                if self.dup_sems is not None:
                    self.dup(distance, sign).start()

    def settle(self, distance):
        for sign in (1, -1) if distance else (1,):
            if distance <= self.hops[sign]:
                self.dup(distance, sign, True).wait_recv()

    def drain(self):
        for sign in (1, -1):
            for distance in range(1, self.hops[sign] + 1):
                self.copy(distance, sign, False).wait_send()
                if self.dup_sems is not None:
                    self.dup(distance, sign).wait_send()
        if self.dup_sems is not None:
            self.dup(0, 1).wait_send()


def turn(values, cosine, sine, lane):
    swapped = jnp.where(lane % HEAD < HEAD // 2, pltpu.roll(values, 2 * HEAD - HEAD // 2, 1), pltpu.roll(values, HEAD // 2, 1))
    return values * cosine + swapped * sine


def layer_kernel(n, hidden_ref, idx_ref, count_ref, norm_ref, router_ref, wq_ref, wk_ref, wv_ref,
                 wo_ref, gain_ref, rate_ref, final_ref,
                 normed_buf, meta_buf, metas_buf, x_buf, kvw_own, kvw_buf, wq_buf, wo_buf, q_acc, q_buf,
                 kv_own, kv_buf, pairs_buf, mask_buf, att_buf, out_buf, update_buf, cos_buf, sin_buf,
                 rows_send, rows_recv, meta_send, meta_recv, att_send, att_recv, out_send, out_recv,
                 w_send, w_recv, dup_send, dup_recv, a_send, a_recv):
    ring = Ring(n)
    chips, chip, core, group, me = ring.chips, ring.chip, ring.core, ring.group, ring.me
    other = 1 - group
    barrier = pltpu.get_barrier_semaphore()
    for device in ({"blk": ring.ahead}, {"blk": ring.behind}, {"blk": ring.partner},
                   {"groups": other}, {"groups": other, "blk": ring.partner}):
        pl.semaphore_signal(barrier, inc=1, device_id=device, device_id_type=MESH)
    tokens, width = hidden_ref.shape
    cap = idx_ref.shape[1]
    lanes = 2 * HEAD
    half = width // 2
    part = half // 2
    slots = 2 * cap
    keep = pairs_buf.shape[0]
    home_here = core == group

    def side(ref):
        return jnp.where(group == 0, ref[:, :HEAD].astype(jnp.float32), ref[:, HEAD:].astype(jnp.float32))

    kvw_own[...] = jnp.concatenate([side(wk_ref), side(wv_ref)], axis=1).astype(jnp.bfloat16)
    line = lax.broadcasted_iota(jnp.int32, meta_buf.shape, 0)
    meta_buf[...] = jnp.where(line == 0, idx_ref[...], count_ref[...])

    def columns(ref, k):
        return ref.at[:, pl.ds(pl.multiple_of(group * half + k * part, part), part)]

    rows_each = wq_ref.shape[0]
    kvw = Spread(ring, kvw_own, kvw_buf, rows_each, (w_send.at[0], w_recv.at[0]), (dup_send.at[0], dup_recv.at[0]))
    wq = [Spread(ring, columns(wq_ref, k), wq_buf.at[k], rows_each, (w_send.at[1 + k], w_recv.at[1 + k]),
                 (dup_send.at[1 + k], dup_recv.at[1 + k]), flip=k == 1) for k in range(2)]
    wo = [Spread(ring, columns(wo_ref, k), wo_buf.at[k], rows_each, (w_send.at[3 + k], w_recv.at[3 + k]),
                 (dup_send.at[3 + k], dup_recv.at[3 + k]), flip=k == 1) for k in range(2)]
    kv = Spread(ring, kv_own, kv_buf, slots, (a_send.at[0], a_recv.at[0]))
    own_metas = metas_buf.at[pl.ds(pl.multiple_of(chip * 2, 2), 2)]
    metas = Spread(ring, own_metas, metas_buf, 2, (a_send.at[1], a_recv.at[1]), flip=True)

    def to_seq(k):
        target = chip * 2 + group
        return {"blk": target} if k == 0 else {"groups": other, "blk": target}

    def rows_copy(k, j):
        return pltpu.make_async_remote_copy(
            src_ref=normed_buf, dst_ref=x_buf.at[j], send_sem=rows_send.at[k], recv_sem=rows_recv.at[j],
            device_id=to_seq(k), device_id_type=MESH)

    def meta_copy(k, j):
        return pltpu.make_async_remote_copy(
            src_ref=meta_buf, dst_ref=metas_buf.at[chip * 2 + j], send_sem=meta_send.at[k], recv_sem=meta_recv.at[j],
            device_id=to_seq(k), device_id_type=MESH)

    pl.semaphore_wait(barrier, 5)
    kvw.start()
    wq[0].start()
    wq[1].start()
    meta_copy(1, core).start()

    @pl.when(home_here)
    def _():
        metas_buf[chip * 2 + core] = meta_buf[...]

    @pl.when(jnp.logical_not(home_here))
    def _():
        meta_copy(0, core).start()

    pick = lax.broadcasted_iota(jnp.int32, (tokens, cap), 0) == idx_ref[...]
    token_rows = lax.dot_general(
        pick.astype(jnp.float32).astype(jnp.bfloat16),
        hidden_ref[...],
        (((0,), (0,)), ((), ())),
        preferred_element_type=jnp.float32,
    )
    final_ref[...] = token_rows.astype(jnp.bfloat16)
    normed_buf[...] = rms_scale(token_rows, norm_ref[...]).astype(jnp.bfloat16)
    rows_copy(1, core).start()

    @pl.when(home_here)
    def _():
        x_buf[core] = normed_buf[...]

    @pl.when(jnp.logical_not(home_here))
    def _():
        rows_copy(0, core).start()

    def arrived(copy):
        for j in range(2):
            @pl.when(jnp.logical_not(jnp.logical_and(home_here, core == j)))
            def _():
                copy(1, j).wait_recv()

    kvw.serve(1)
    arrived(meta_copy)
    metas.start()
    wq[0].serve(1)
    wq[1].serve(1)
    kvw.serve(2)
    metas.serve(1)
    kvw.serve(3)
    metas.serve(2)
    kvw.serve(4)
    metas.serve(3)
    wq[0].serve(2)
    wq[1].serve(2)
    metas.serve(4)
    for d in range(chips // 2 + 1):
        kvw.settle(d)

    lane = lax.broadcasted_iota(jnp.int32, (1, lanes), 1)
    sign = jnp.where(lane % HEAD < HEAD // 2, -1.0, 1.0)
    square_row = lax.broadcasted_iota(jnp.int32, (cap, cap), 0)
    square_col = lax.broadcasted_iota(jnp.int32, (cap, cap), 1)
    slot = lax.broadcasted_iota(jnp.int32, (1, cap), 1)
    for j in range(2):
        spots = (metas_buf[chip * 2 + j, 0:1, :] + (chip * 2 + j) * tokens).astype(jnp.float32)
        spot = jnp.sum(jnp.where(square_row == square_col, spots, 0.0), axis=1, keepdims=True)
        angle = spot * rate_ref[...]
        cos_buf[j * cap : (j + 1) * cap, :] = jnp.cos(angle)
        sin_buf[j * cap : (j + 1) * cap, :] = jnp.sin(angle) * sign
    starts, counts = [], []
    start = jnp.zeros((1, cap), jnp.int32)
    own_start = [jnp.zeros((1, cap), jnp.int32) for _ in range(2)]
    for s in range(n):
        count = metas_buf[s, 1:2, :]
        starts.append(start)
        counts.append(count)
        start = start + count
        for j in range(2):
            own_start[j] = own_start[j] + jnp.where(chip * 2 + j > s, count, 0)
    for j in range(2):
        for k in range(keep // cap):
            seen = square_col + k * cap - square_row <= own_start[j]
            mask_buf[j * cap : (j + 1) * cap, k * cap : (k + 1) * cap] = jnp.where(seen, 0.0, -1e30)

    arrived(rows_copy)
    kvw_buf[pl.ds(pl.multiple_of(me * rows_each, rows_each), rows_each)] = kvw_own[...]
    x_all = x_buf[...].reshape(slots, width)
    both = jnp.dot(x_all, kvw_buf[...], preferred_element_type=jnp.float32)
    gain = jnp.concatenate([gain_ref[1:2, :], gain_ref[1:2, :]], axis=1)
    mean = jnp.sum(jnp.where(lane < HEAD, both * both, 0.0), axis=1, keepdims=True) * (1.0 / HEAD)
    key = turn(both * lax.rsqrt(mean + norm_eps) * gain, cos_buf[...], sin_buf[...], lane)
    kv_own[...] = jnp.where(lane < HEAD, key, both).astype(jnp.bfloat16)
    kv.start()
    kv_buf[pl.ds(pl.multiple_of(chip * slots, slots), slots)] = kv_own[...]

    def own_rows(ref, buf, k):
        buf[k, pl.ds(pl.multiple_of(me * rows_each, rows_each), rows_each)] = columns(ref, k)[...]

    def q_block(distance, sgn):
        at = ring.chip_at(ring.place - sgn * distance) * (2 * rows_each)
        at = pl.ds(pl.multiple_of(at, 2 * rows_each), 2 * rows_each)
        source = x_buf[:, :, at].reshape(slots, 2 * rows_each)
        for k in range(2):
            cols = slice(k * part, (k + 1) * part)
            product = jnp.dot(source, wq_buf[k, at, :], preferred_element_type=jnp.float32)
            q_acc[:, cols] = product if distance == 0 else q_acc[:, cols] + product

    def q_wave(distance):
        for k in range(2):
            wq[k].settle(distance)
        for sgn in (1, -1) if 0 < distance < chips // 2 else (1,):
            q_block(distance, sgn)

    for k in range(2):
        own_rows(wq_ref, wq_buf, k)
        own_rows(wo_ref, wo_buf, k)
    q_wave(0)
    q_wave(1)
    wq[0].serve(3)
    wq[1].serve(3)
    wo[0].start()
    wo[1].start()
    kv.serve(1)
    q_wave(2)
    wq[0].serve(4)
    wq[1].serve(4)
    q_wave(3)
    kv.serve(2)
    q_wave(4)

    gain = jnp.concatenate([gain_ref[0:1, :], gain_ref[0:1, :]], axis=1) * (1.0 / math.sqrt(HEAD))

    def q_finish(p):
        total = q_acc[:, p * lanes : (p + 1) * lanes]
        squares = total * total
        first = jnp.sum(jnp.where(lane < HEAD, squares, 0.0), axis=1, keepdims=True)
        second = jnp.sum(jnp.where(lane < HEAD, 0.0, squares), axis=1, keepdims=True)
        mean = jnp.where(lane < HEAD, first, second) * (1.0 / HEAD)
        values = total * lax.rsqrt(mean + norm_eps) * gain
        values = turn(values, cos_buf[...], sin_buf[...], lane)
        q_buf[2 * p] = jnp.where(lane < HEAD, values, 0.0).astype(jnp.bfloat16)
        q_buf[2 * p + 1] = jnp.where(lane < HEAD, pltpu.roll(values, HEAD, 1), 0.0).astype(jnp.bfloat16)

    heads = half // HEAD
    for p in range(heads // 2):
        q_finish(p)
    wo[0].serve(1)
    wo[1].serve(1)
    kv.serve(3)
    kv.serve(4)
    blocks = keep // cap
    for k in range(blocks):
        begin, end = k, min(n, k + n - blocks + 1)
        hits = []
        for s in range(begin, end):
            ranks = jnp.where(slot < counts[s], starts[s] + slot, -1)
            hits.append((square_row + k * cap == ranks).astype(jnp.float32).astype(jnp.bfloat16))
        dense = jnp.dot(jnp.concatenate(hits, axis=1), kv_buf[begin * cap : end * cap, :], preferred_element_type=jnp.float32)
        pairs_buf[k * cap : (k + 1) * cap, :] = dense.astype(jnp.bfloat16)

    def attend_head(h):
        scores = lax.dot_general(
            q_buf[h], pairs_buf[...], (((1,), (1,)), ((), ())), preferred_element_type=jnp.float32
        ) + mask_buf[...]
        top = jnp.max(scores, axis=-1, keepdims=True)
        weights = jnp.exp(scores - top)
        denominator = jnp.sum(weights, axis=-1, keepdims=True)
        mix = jnp.dot(weights.astype(jnp.bfloat16), pairs_buf[...], preferred_element_type=jnp.float32)
        return mix / denominator

    def att_copy(i, source):
        at = att_buf.at[source * (chips // 2) + i]
        return pltpu.make_async_remote_copy(
            src_ref=at, dst_ref=at, send_sem=att_send.at[i], recv_sem=att_recv.at[i],
            device_id={"groups": other}, device_id_type=MESH)

    chunk_heads = heads // (chips // 2)
    for i in range(chips // 2):
        for p in range(chunk_heads // 2):
            mixes = [attend_head(i * chunk_heads + 2 * p + e) for e in range(2)]
            joined = jnp.where(lane < HEAD, pltpu.roll(mixes[0], HEAD, 1), mixes[1])
            att_buf[group * (chips // 2) + i, :, p * lanes : (p + 1) * lanes] = joined.astype(jnp.bfloat16)
        att_copy(i, group).start()
        if i + 2 <= chips // 2:
            wo[0].serve(i + 2)
            wo[1].serve(i + 2)

    for i in range(chips // 2):
        att_copy(i, other).wait_recv()
    for k in range(2):
        for d in range(chips // 2 + 1):
            wo[k].settle(d)

    def out_copy(k, j, here):
        target = chip * 2 + j
        return pltpu.make_async_remote_copy(
            src_ref=out_buf.at[k, j], dst_ref=update_buf.at[group, k], send_sem=out_send.at[k, j], recv_sem=out_recv.at[group, k],
            device_id={"blk": target} if here else {"groups": other, "blk": target}, device_id_type=MESH)

    for k in range(2):
        total = None
        for i in range(chips):
            product = jnp.dot(att_buf[i], wo_buf[k, i * 2 * rows_each : (i + 1) * 2 * rows_each, :], preferred_element_type=jnp.float32)
            total = product if total is None else total + product
        out_buf[k] = total.astype(jnp.bfloat16).reshape(2, cap, part)

        @pl.when(home_here)
        def _():
            update_buf[group, k] = out_buf[k, core]
            out_copy(k, 1 - core, True).start()

        @pl.when(jnp.logical_not(home_here))
        def _():
            for j in range(2):
                out_copy(k, j, False).start()

    rows = final_ref[...].astype(jnp.float32)
    gate = jax.nn.sigmoid(jnp.sum(rows * router_ref[...].astype(jnp.float32), axis=1, keepdims=True))

    def update_wait(h, k):
        pltpu.make_async_remote_copy(
            src_ref=out_buf.at[k, 0], dst_ref=update_buf.at[h, k], send_sem=out_send.at[k, 0], recv_sem=out_recv.at[h, k],
            device_id={"groups": other}, device_id_type=MESH).wait_recv()

    for k in range(2):
        update_wait(other, k)

        @pl.when(jnp.logical_not(home_here))
        def _():
            update_wait(group, k)

        for h in range(2):
            cols = slice(h * half + k * part, h * half + (k + 1) * part)
            final_ref[:, cols] = (rows[:, cols] + gate * update_buf[h, k].astype(jnp.float32)).astype(jnp.bfloat16)

    for item in [kvw, kv, metas] + wq + wo:
        item.drain()
    for i in range(chips // 2):
        att_copy(i, group).wait_send()
    rows_copy(1, core).wait_send()
    meta_copy(1, core).wait_send()

    @pl.when(home_here)
    def _():
        for k in range(2):
            out_copy(k, 1 - core, True).wait_send()

    @pl.when(jnp.logical_not(home_here))
    def _():
        rows_copy(0, core).wait_send()
        meta_copy(0, core).wait_send()
        for k in range(2):
            for j in range(2):
                out_copy(k, j, False).wait_send()


def layer(n, keep, hidden, kept_idx, kept_count, router, norm_gain, qk_gain, query_weight, key_weight,
          value_weight, out_weight):
    tokens, width = hidden.shape
    cap = kept_idx.shape[1]
    lanes, chips = 2 * HEAD, n // 2
    half, part, slots = width // 2, width // 4, 2 * cap
    rows_each = query_weight.shape[0]
    half_size = HEAD // 2
    rates = rope_base ** (-(np.arange(half_size) * 2.0 / HEAD))
    rates = np.tile(rates, lanes // half_size)[None, :].astype(np.float32)
    dma = pltpu.SemaphoreType.DMA
    return pl.pallas_call(
        functools.partial(layer_kernel, n),
        out_shape=jax.ShapeDtypeStruct((cap, width), jnp.bfloat16),
        in_specs=[VM] * 11,
        out_specs=VM,
        scratch_shapes=[
            pltpu.VMEM((cap, width), jnp.bfloat16),
            pltpu.VMEM((8, cap), jnp.int32),
            pltpu.VMEM((n, 8, cap), jnp.int32),
            pltpu.VMEM((2, cap, width), jnp.bfloat16),
            pltpu.VMEM((rows_each, lanes), jnp.bfloat16),
            pltpu.VMEM((width, lanes), jnp.bfloat16),
            pltpu.VMEM((2, width, part), jnp.bfloat16),
            pltpu.VMEM((2, width, part), jnp.bfloat16),
            pltpu.VMEM((slots, half), jnp.float32),
            pltpu.VMEM((half // HEAD, slots, lanes), jnp.bfloat16),
            pltpu.VMEM((slots, lanes), jnp.bfloat16),
            pltpu.VMEM((n * cap, lanes), jnp.bfloat16),
            pltpu.VMEM((keep, lanes), jnp.bfloat16),
            pltpu.VMEM((slots, keep), jnp.float32),
            pltpu.VMEM((chips, slots, width // chips), jnp.bfloat16),
            pltpu.VMEM((2, 2, cap, part), jnp.bfloat16),
            pltpu.VMEM((2, 2, cap, part), jnp.bfloat16),
            pltpu.VMEM((slots, lanes), jnp.float32),
            pltpu.VMEM((slots, lanes), jnp.float32),
            dma((2,)), dma((2,)), dma((2,)), dma((2,)),
            dma((chips // 2,)), dma((chips // 2,)), dma((2, 2)), dma((2, 2)),
        ]
        + Spread.semaphores(chips, 5)
        + [dma((5, chips)), dma((5, chips))]
        + Spread.semaphores(chips, 2),
        compiler_params=pltpu.CompilerParams(collective_id=1, has_side_effects=True),
    )(
        hidden, kept_idx, kept_count.reshape(1, 1), norm_gain.reshape(1, width), router.reshape(1, width),
        query_weight, key_weight, value_weight, out_weight, qk_gain, rates,
    )


def body(
    n,
    hidden,
    kept_idx,
    kept_count,
    router,
    norm_gain,
    qk_gain,
    query_weight,
    key_weight,
    value_weight,
    out_weight,
):
    tokens = hidden.shape[0]
    cap = kept_idx.shape[1]
    keep = n * (tokens * KEEP_DEV // TOK_DEV)
    final = layer(
        n, keep, hidden, kept_idx, kept_count, router, norm_gain, qk_gain, query_weight, key_weight,
        value_weight, out_weight,
    )
    slots = jnp.arange(cap, dtype=jnp.int32)
    put = (kept_idx == jnp.arange(tokens, dtype=jnp.int32)[:, None]) & (slots[None, :] < kept_count[0])
    placed = jnp.dot(put.astype(jnp.bfloat16), final, preferred_element_type=jnp.float32)
    return jnp.where(jnp.any(put, axis=1)[:, None], placed.astype(jnp.bfloat16), hidden)


def attend(query_heads, query_ranks, key_block, value_block, key_ranks, state):
    prev_top, prev_total, prev_acc = state
    length = key_block.shape[0]
    keys_split = key_block.reshape(length, KV_HEADS, HEAD)
    values_split = value_block.reshape(length, KV_HEADS, HEAD)
    scores = jnp.einsum(
        "agch,bgh->gcab", query_heads, keys_split, preferred_element_type=jnp.float32
    ) * (1.0 / math.sqrt(HEAD))
    allowed = key_ranks[None, :] <= query_ranks[:, None]
    masked = jnp.where(allowed, scores, -1e30)
    new_top = jnp.maximum(prev_top, jnp.max(masked, axis=-1))
    weights = jnp.where(allowed, jnp.exp(masked - new_top[..., None]), 0.0)
    factor = jnp.exp(prev_top - new_top)
    new_total = prev_total * factor + jnp.sum(weights, axis=-1)
    new_acc = prev_acc * factor[..., None] + jnp.einsum(
        "gcab,bgh->gcah",
        weights.astype(jnp.bfloat16),
        values_split,
        preferred_element_type=jnp.float32,
    )
    return (new_top, new_total, new_acc)


def make_fold(query_heads, query_ranks, rank_of, state, pieces):
    key_piece, value_piece = pieces
    length = key_piece.shape[0]

    def inner(block_turn, inner_state):
        block_start = block_turn * 512
        key_block = lax.dynamic_slice_in_dim(key_piece, block_start, 512, 0)
        value_block = lax.dynamic_slice_in_dim(value_piece, block_start, 512, 0)
        key_ranks = rank_of(block_start + jnp.arange(512, dtype=jnp.int32))
        return attend(query_heads, query_ranks, key_block, value_block, key_ranks, inner_state)

    return lax.fori_loop(0, length // 512, inner, state)


def wide_body(
    hidden,
    kept_idx,
    kept_count,
    router,
    norm_gain,
    qk_gain,
    query_weight,
    key_weight,
    value_weight,
    out_weight,
):
    shard_count = lax.axis_size("blk")
    device = lax.axis_index("blk")
    width = hidden.shape[1]
    all_lists, all_counts = (
        lax.all_gather(kept_idx, "blk", axis=0, tiled=True),
        lax.all_gather(kept_count, "blk", axis=0, tiled=True),
    )
    starts = jnp.cumsum(all_counts) - all_counts
    own_start = starts[device]
    own_count = all_counts[device]
    list_slots = jnp.arange(CAP, dtype=jnp.int32)
    is_valid = list_slots < own_count
    token_rows = hidden[kept_idx[0]]
    gate_value = jax.nn.sigmoid(jnp.dot(token_rows, router, preferred_element_type=jnp.float32))
    slot_count = (CAP + shard_count - 1) // shard_count
    outgoing = jnp.where(is_valid[:, None], token_rows, jnp.zeros_like(token_rows))
    outgoing = jnp.roll(outgoing.reshape(slot_count, shard_count, width), own_start, axis=1)
    incoming = lax.all_to_all(outgoing, "blk", split_axis=1, concat_axis=1, tiled=True)
    query_ranks = device + jnp.arange(KEEP_DEV, dtype=jnp.int32) * shard_count
    source_ends = starts + all_counts
    source = jnp.sum((source_ends[None, :] <= query_ranks[:, None]).astype(jnp.int32), axis=1)
    within = query_ranks - starts[source]
    flat_index = within // shard_count * shard_count + source
    kept_rows = incoming.reshape(slot_count * shard_count, width)[flat_index]
    positions = source * TOK_DEV + all_lists[source, within]
    row_total = kept_rows.shape[0]
    normed = rms_scale(kept_rows.astype(jnp.float32), norm_gain).astype(jnp.bfloat16)
    query_cols = Q_HEADS * HEAD
    kv_cols = KV_HEADS * HEAD
    full_query, full_key, full_value, full_out = (
        lax.all_gather(query_weight, "blk", axis=0, tiled=True),
        lax.all_gather(key_weight, "blk", axis=0, tiled=True),
        lax.all_gather(value_weight, "blk", axis=0, tiled=True),
        lax.all_gather(out_weight, "blk", axis=0, tiled=True),
    )
    query_lin = jnp.dot(normed, full_query, preferred_element_type=jnp.float32)
    key_lin = jnp.dot(normed, full_key, preferred_element_type=jnp.float32)
    value_lin = jnp.dot(normed, full_value, preferred_element_type=jnp.float32)
    half_size = HEAD // 2
    rotation_rates = rope_base ** (-(jnp.arange(half_size, dtype=jnp.float32) * 2.0 / HEAD))
    angles = (positions.astype(jnp.float32)[:, None] * rotation_rates[None, :])[:, None, :]
    query_heads = rotate(
        rms_scale(query_lin.reshape(row_total, Q_HEADS, HEAD), qk_gain[0]), angles
    ).astype(jnp.bfloat16)
    key_heads = rotate(
        rms_scale(key_lin.reshape(row_total, KV_HEADS, HEAD), qk_gain[1]), angles
    ).astype(jnp.bfloat16)
    query_heads = query_heads.reshape(row_total, KV_HEADS, Q_HEADS // KV_HEADS, HEAD)
    key_flat = key_heads.reshape(row_total, kv_cols)
    value_flat = value_lin.astype(jnp.bfloat16)
    group_size = Q_HEADS // KV_HEADS
    start_state = (
        jnp.full((KV_HEADS, group_size, row_total), -1e30, jnp.float32),
        jnp.zeros((KV_HEADS, group_size, row_total), jnp.float32),
        jnp.zeros((KV_HEADS, group_size, row_total, HEAD), jnp.float32),
    )

    def strided_rank(slots_seen):
        return slots_seen // KEEP_DEV + slots_seen % KEEP_DEV * shard_count

    final_top, final_total, final_acc = make_fold(
        query_heads,
        query_ranks,
        strided_rank,
        start_state,
        (
            lax.all_gather(key_flat, "blk", axis=0, tiled=True),
            lax.all_gather(value_flat, "blk", axis=0, tiled=True),
        ),
    )
    attended = (
        (final_acc / final_total[..., None])
        .transpose(2, 0, 1, 3)
        .reshape(row_total, query_cols)
        .astype(jnp.bfloat16)
    )
    update = jnp.dot(attended, full_out, preferred_element_type=jnp.float32)
    update = update.astype(jnp.bfloat16)
    slot_grid = (
        jnp.arange(slot_count, dtype=jnp.int32)[:, None] * shard_count
        + jnp.mod(device - starts, shard_count)[None, :]
    )
    back_valid = slot_grid < all_counts[None, :]
    local_place = (starts[None, :] + slot_grid - device) // shard_count
    clipped = jnp.where(back_valid, local_place, 0)
    back_rows = jnp.where(back_valid[..., None], update[clipped], jnp.zeros((), jnp.bfloat16))
    returned = lax.all_to_all(back_rows, "blk", split_axis=1, concat_axis=1, tiled=True)
    returned = jnp.roll(returned, -own_start, axis=1).reshape(slot_count * shard_count, width)
    final = (
        token_rows.astype(jnp.float32) + gate_value[:, None] * returned.astype(jnp.float32)
    ).astype(jnp.bfloat16)
    target = jnp.where(is_valid, kept_idx[0], TOK_DEV)
    return hidden.at[target].set(final, mode="drop")


def solution(mesh):
    placed = (
        P(("groups", "blk"), None),
        P(("groups", "blk"), None),
        P(("groups", "blk")),
        P(),
        P(),
        P(),
        P("blk", None),
        P("blk", None),
        P("blk", None),
        P("blk", None),
    )
    n = mesh.shape["blk"]
    by_heads = n % 4 == 0 and Q_HEADS == 2 * n and mesh.shape["groups"] == KV_HEADS
    step = functools.partial(body, n) if by_heads else wide_body
    return jax.shard_map(
        step, mesh=mesh, in_specs=placed, out_specs=P(("groups", "blk"), None), check_vma=False
    )
```

time: 117 us -> 91.5 us (0.78)
  Pallas kernels: 110 us -> 85.3 us
    pallas_call x1, Pallas kernels: 110 us -> 85.3 us  [layer(): pl.pallas_call(functools.partial(layer_kernel, n), out_shape=jax.ShapeDty...]
where the time goes in v1:
time: 91.5 us; the launch traced here: 91.3 us
  Pallas kernels  85.3 us (93%)
  matrix products  3.07 us (3%)
  local copies, waits for them, and re-layouts  1.31 us (1%)
    pallas_call x1, Pallas kernels, layer(): pl.pallas_call(functools.partial(layer_kernel, n), out_shape=jax.ShapeDty...  85.3 us
    dot_general x1, matrix products, body(): jnp.dot(put.astype(jnp.bfloat16), final, preferred_element_type=jnp.float32)  3.07 us

profile of v1, /device:TPU:1, one launch (start us, length us, event | category | flops | bytes accessed | tf_op | source)
XLA Modules:
  0.0 91.3 jit_solution(9768678480445380928)
XLA Ops:
  0.0 0.0 copy-start.1
  0.0 0.0 copy-start
  0.8 0.8 fusion.3
  1.6 1.3 %reshape.17.router_ref = bf16[1,2048]{1,0:T(2,128)(2,1)} reshape(bf16[2048]{0:T(1024)(128)(2,1)} %param.14) | data formatting | bytes 8192 | tf_op jit(solution)/shard_map/reshape | solution.py:499
  2.9 85.3 %shard_map.109 = bf16[128,2048]{1,0:T(8,128)(2,1)} custom-call(bf16[512,2048]{1,0:T(8,128)(2,1)} %hidden_ref.1, s32[1,128]{1,0:T(1,128)} %idx_ref.1, s32[1,1]{1,0:T(1,128)} %bitcast.6.count_ref, f32[1,2048]{1,0:T(1,128)} %bitcast.7, bf16[1,2048]{1,0:T(2,128)(2,1)} %reshape.17.router_ref, bf16[128,2048]{1,0:T(8,128)(2,1)} %wq_ref.1, bf16[128,128]{1,0:T(8,128)(2,1)} %wk_ref.1, ...), custom_call_target="tpu_custom_call" | custom-call | tf_op jit(solution)/shard_map/pallas_call | solution.py:466
  88.2 0.0 copy-done.1
  88.2 0.0 copy-done
  88.2 3.1 %fusion = bf16[512,2048]{1,0:T(8,128)(2,1)} fusion(bf16[512,2048]{1,0:T(8,128)(2,1)S(1)} %copy-done, bf16[128,2048]{1,0:T(8,128)(2,1)} %shard_map.109, pred[512]{0:T(512)(128)(4,1)S(1)} %fusion.3, s32[128]{0:T(128)S(1)} %bitcast.9, pred[128]{0:T(512)(128)(4,1)S(1)} %iota_compare_fusion.1), kind=kOutput, calls=%fused_computation.1 | convolution fusion | flops 270663680 | bytes 4719744 | tf_op jit(solution)/shard_map/dot_general | solution.py:526
  (1 shorter events, 0.0 us)
Async XLA Ops:
  0.0 88.2 %copy-start.1 = (s32[1,128]{1,0:T(1,128)S(1)}, s32[1,128]{1,0:T(1,128)}, u32[]{:S(2)}) copy-start(s32[1,128]{1,0:T(1,128)} %idx_ref.1) | copy-start | bytes 1540
  0.0 88.2 %copy-start = (bf16[512,2048]{1,0:T(8,128)(2,1)S(1)}, bf16[512,2048]{1,0:T(8,128)(2,1)}, u32[]{:S(2)}) copy-start(bf16[512,2048]{1,0:T(8,128)(2,1)} %hidden_ref.1) | copy-start | bytes 6291460

commit v2 on v1

v2 whole, which is shorter than its diff:
```python
import functools
import math

import jax
import jax.numpy as jnp
import numpy as np
from jax import lax
from jax.experimental import pallas as pl
from jax.experimental.pallas import tpu as pltpu
from jax.sharding import PartitionSpec as P

Q_HEADS = 32
KV_HEADS = 2
HEAD = 64
TOK_DEV = 512
KEEP_DEV = 64
CAP = 128
MESH = pl.DeviceIdType.MESH
ANY = pl.BlockSpec(memory_space=pl.ANY)
HBM = pl.BlockSpec(memory_space=pltpu.HBM)


norm_eps = 1e-06
rope_base = 1000000.0


def rms_scale(values, scales):
    return values * lax.rsqrt(jnp.mean(values * values, axis=-1, keepdims=True) + norm_eps) * scales


def rotate(values, angles):
    half_size = values.shape[-1] // 2
    lower_half = values[..., :half_size]
    upper_half = values[..., half_size:]
    cosine = jnp.cos(angles)
    sine_part = jnp.sin(angles)
    return jnp.concatenate(
        [
            lower_half * cosine - upper_half * sine_part,
            upper_half * cosine + lower_half * sine_part,
        ],
        axis=-1,
    )


class Place:
    def __init__(self, n):
        self.depth = n // 4
        self.me = lax.axis_index("blk")
        self.group = lax.axis_index("groups")
        self.chip, self.core = self.me // 2, self.me % 2
        self.z, self.y = self.chip // 2, self.chip % 2
        self.partner = self.chip * 2 + 1 - self.core
        self.across = (self.chip + 1 - 2 * self.y) * 2

    def inside(self, z):
        return jnp.logical_and(z >= 0, z < self.depth)


def remote(source, target, send, recv, device):
    return pltpu.make_async_remote_copy(
        src_ref=source, dst_ref=target, send_sem=send, recv_sem=recv, device_id=device, device_id_type=MESH
    )


class Line:
    direct = True

    def __init__(self, place, own, buf, rows, view, sems):
        self.place, self.own, self.buf, self.rows, self.view = place, own, buf, rows, view
        self.z_send, self.z_recv, self.dup_send, self.dup_recv = sems
        self.dups = place.depth

    @staticmethod
    def semaphores(depth, count):
        dma = pltpu.SemaphoreType.DMA
        return [dma((count,)), dma((count, depth)), dma((count,)), dma((count,))]

    def along(self, source, z, offset):
        p = self.place
        return remote(source, self.view(z, p.core), self.z_send, self.z_recv.at[z], {"blk": p.me + 4 * offset})

    def dup(self, source, target):
        return remote(source, target, self.dup_send, self.dup_recv, {"blk": self.place.partner})

    def launch(self, source):
        p = self.place
        for offset in range(1, p.depth if self.direct else 2):
            for sign in (1, -1):
                @pl.when(p.inside(p.z + sign * offset))
                def _():
                    self.along(source, p.z, sign * offset).start()

    def start(self):
        p = self.place
        self.launch(self.own)
        self.dup(self.own, self.view(p.z, p.core)).start()

    def passed(self, z):
        pass

    def serve(self, distance):
        p = self.place
        for sign in (1, -1):
            z = p.z - sign * distance

            @pl.when(p.inside(z))
            def _():
                block = self.view(z, p.core)
                self.along(block, z, sign).wait_recv()
                if not self.direct:
                    @pl.when(p.inside(p.z + sign))
                    def _():
                        self.along(block, z, sign).start()

                self.passed(z)
                self.dup(block, block).start()

    def serve_all(self):
        for distance in range(1, self.place.depth):
            self.serve(distance)

    def total(self, blocks):
        return self.buf.at[pl.ds(0, blocks * self.rows)]

    def settle(self):
        whole = self.total(self.dups)
        self.dup(whole, whole).wait_recv()

    def drain(self):
        p = self.place

        def sent(blocks):
            whole = self.total(blocks)
            remote(whole, whole, self.z_send, self.z_recv.at[0], {"blk": p.partner}).wait_send()

        if self.direct:
            sent(p.depth - 1)
        else:
            middle = jnp.logical_and(p.z > 0, p.z < p.depth - 1)
            pl.when(middle)(lambda: sent(p.depth + 1))
            pl.when(jnp.logical_not(middle))(lambda: sent(1))
        whole = self.total(self.dups)
        self.dup(whole, whole).wait_send()


class Weight(Line):
    def __init__(self, place, mine, theirs, buf, sems, direct=False):
        self.place, self.mine, self.theirs, self.buf, self.direct = place, mine, theirs, buf, direct
        self.rows = mine.shape[0]
        self.z_send, self.z_recv, self.dup_send, self.dup_recv = sems[:4]
        self.side_recv, self.side_send, self.x_recv = sems[4:]
        self.dups = 2 * place.depth

    @staticmethod
    def semaphores(depth, count):
        dma = pltpu.SemaphoreType.DMA
        return Line.semaphores(depth, count) + [dma((count,)), dma((count,)), dma((count, depth))]

    def block(self, z, y, core):
        at = (4 * z + 2 * y + core) * self.rows
        return self.buf.at[pl.ds(pl.multiple_of(at, self.rows), self.rows)]

    def view(self, z, core):
        return self.block(z, self.place.group, core)

    def side(self, y):
        p = self.place
        return remote(self.theirs, self.block(p.z, y, p.core), self.side_send, self.side_recv, {"blk": p.across + p.core})

    def other(self, z, group):
        block = self.block(z, group, self.place.core)
        return remote(block, block, self.side_send, self.x_recv.at[z], {"groups": 1 - self.place.group})

    def start_side(self):
        self.side(self.place.y).start()

    def start(self):
        p = self.place

        @pl.when(p.y == p.group)
        def _():
            self.launch(self.mine)

        self.dup(self.mine, self.block(p.z, p.y, p.core)).start()

    def keep(self, sem):
        p = self.place
        return pltpu.make_async_copy(self.mine, self.block(p.z, p.y, p.core), sem)

    def sided(self):
        p = self.place
        block = self.block(p.z, 1 - p.y, p.core)
        self.side(1 - p.y).wait_recv()

        @pl.when(p.y != p.group)
        def _():
            self.launch(block)

        self.dup(block, block).start()

    def passed(self, z):
        self.other(z, self.place.group).start()

    def cross(self, distance):
        p = self.place
        for sign in (1, -1):
            z = p.z - sign * distance

            @pl.when(p.inside(z))
            def _():
                self.other(z, 1 - p.group).wait_recv()
                block = self.block(z, 1 - p.group, p.core)
                self.dup(block, block).start()

    def cross_all(self):
        for distance in range(1, self.place.depth):
            self.cross(distance)

    def drain(self):
        super().drain()
        whole = self.total(self.place.depth)
        remote(whole, whole, self.side_send, self.side_recv, {"blk": self.place.partner}).wait_send()


def turn(values, cosine, sine, lane):
    swapped = jnp.where(lane % HEAD < HEAD // 2, pltpu.roll(values, 2 * HEAD - HEAD // 2, 1), pltpu.roll(values, HEAD // 2, 1))
    return values * cosine + swapped * sine


def layer_kernel(n, pieces, hidden_ref, wq_ref, wo_ref, idx_hbm, count_hbm, norm_hbm, router_hbm, wk_hbm, wv_hbm,
                 gain_hbm, rate_hbm, out_ref, idx_ref, count_ref, norm_ref, router_ref, wk_ref, wv_ref, gain_ref, rate_ref,
                 small_sem, final_ref, placed_buf, placed_sem,
                 normed_buf, meta_buf, metas_buf, x_buf, kvw_own, kvw_buf, wq_buf, wo_buf, q_buf,
                 kv_own, kv_buf, pairs_buf, mask_buf, att_buf, out_buf, update_buf, cos_buf, sin_buf,
                 rows_send, rows_recv, meta_send, meta_recv, att_send, att_recv, out_send, out_recv, keep_sem, load_sem, hidden_buf, *sems):
    p = Place(n)
    depth, chip, core, y, me = p.depth, p.chip, p.core, p.y, p.me
    chips = n // 2
    barrier = pltpu.get_barrier_semaphore()
    for device in ({"blk": p.partner}, {"blk": p.across}, {"blk": p.across + 1}, {"groups": 1 - p.group}):
        pl.semaphore_signal(barrier, inc=1, device_id=device, device_id_type=MESH)
    for offset in range(1, depth):
        for sign in (1, -1):
            @pl.when(p.inside(p.z + sign * offset))
            def _():
                pl.semaphore_signal(barrier, inc=1, device_id={"blk": me + 4 * sign * offset}, device_id_type=MESH)
    load = pltpu.make_async_copy(hidden_ref, hidden_buf, load_sem)
    load.start()
    small = [pltpu.make_async_copy(source, target, small_sem.at[k]) for k, (source, target) in enumerate((
        (idx_hbm, idx_ref), (count_hbm, count_ref), (wk_hbm, wk_ref), (wv_hbm, wv_ref), (norm_hbm, norm_ref),
        (gain_hbm, gain_ref), (rate_hbm, rate_ref), (router_hbm, router_ref)))]
    for copy in small:
        copy.start()
    for item in small:
        item.wait()
    tokens, width = hidden_ref.shape
    cap = idx_ref.shape[1]
    lanes = 2 * HEAD
    half = width // 2
    part = half // pieces
    slots = 2 * cap
    keep = pairs_buf.shape[0]
    home_here = core == y
    away = jnp.logical_not(home_here)
    first_shard = 4 * p.z + 2 * core

    def head_side(ref, of):
        return jnp.where(of == 0, ref[:, :HEAD].astype(jnp.float32), ref[:, HEAD:].astype(jnp.float32))

    for k, of in enumerate((y, 1 - y)):
        kvw_own[k] = jnp.concatenate([head_side(wk_ref, of), head_side(wv_ref, of)], axis=1).astype(jnp.bfloat16)
    line = lax.broadcasted_iota(jnp.int32, meta_buf.shape, 0)
    meta_buf[...] = jnp.where(line == 0, idx_ref[...], count_ref[...])

    def columns(ref, of, k):
        return ref.at[:, pl.ds(pl.multiple_of(of * half + k * part, part), part)]

    rows_each = wq_ref.shape[0]

    def take(sems, i):
        return [s.at[i] for s in sems]

    w_sems, a_sems = sems[:7], sems[7:]
    kvw = Weight(p, kvw_own.at[0], kvw_own.at[1], kvw_buf, take(w_sems, 0), direct=True)
    wq = [Weight(p, columns(wq_ref, y, k), columns(wq_ref, 1 - y, k), wq_buf.at[k], take(w_sems, 1 + k))
          for k in range(pieces)]
    wo = [Weight(p, columns(wo_ref, y, k), columns(wo_ref, 1 - y, k), wo_buf.at[k], take(w_sems, 1 + pieces + k))
          for k in range(pieces)]

    def pair_of(buf, each):
        def view(z, of):
            return buf.at[pl.ds(pl.multiple_of((4 * z + 2 * of) * each, 2 * each), 2 * each)]
        return view

    kv = Line(p, kv_own, kv_buf, slots, pair_of(kv_buf, cap), take(a_sems, 0))
    metas_view = pair_of(metas_buf, 1)
    metas = Line(p, metas_view(p.z, core), metas_buf, 2, metas_view, take(a_sems, 1))

    def worker(k):
        return {"blk": chip * 2 + y if k == 0 else p.across + y}

    def rows_copy(k, j):
        return remote(normed_buf, x_buf.at[j], rows_send.at[k], rows_recv.at[j], worker(k))

    def meta_copy(k, j):
        return remote(meta_buf, metas_buf.at[first_shard_of(k) + j], meta_send.at[k], meta_recv.at[j], worker(k))

    def first_shard_of(k):
        return 4 * p.z + 2 * y

    def meta_wait(k, j):
        return remote(meta_buf, metas_buf.at[first_shard + j], meta_send.at[k], meta_recv.at[j], worker(k))

    def arrived(copy):
        for j in range(2):
            @pl.when(jnp.logical_not(jnp.logical_and(home_here, core == j)))
            def _():
                copy(1, j).wait_recv()

    for item in wq + wo:
        item.keep(keep_sem).start()
    pl.semaphore_wait(barrier, 4 + depth - 1)
    first = wq + [kvw]
    for item in first:
        item.start_side()
    for item in first:
        item.start()
    meta_copy(1, core).start()

    @pl.when(home_here)
    def _():
        metas_buf[first_shard + core] = meta_buf[...]

    @pl.when(away)
    def _():
        meta_copy(0, core).start()

    load.wait()
    pick = lax.broadcasted_iota(jnp.int32, (tokens, cap), 0) == idx_ref[...]
    token_rows = lax.dot_general(
        pick.astype(jnp.float32).astype(jnp.bfloat16),
        hidden_buf[...],
        (((0,), (0,)), ((), ())),
        preferred_element_type=jnp.float32,
    )
    final_ref[...] = token_rows.astype(jnp.bfloat16)
    normed_buf[...] = rms_scale(token_rows, norm_ref[...]).astype(jnp.bfloat16)
    rows_copy(1, core).start()

    @pl.when(home_here)
    def _():
        x_buf[core] = normed_buf[...]

    @pl.when(away)
    def _():
        rows_copy(0, core).start()

    for item in wo:
        item.start_side()
    direct_line = y == p.group

    @pl.when(direct_line)
    def _():
        wq[0].serve(1)
        wq[1].serve(1)
        wq[0].sided()
        wq[2].serve(1)
        wq[1].sided()
        wq[3].serve(1)
        wq[2].sided()
        wq[3].sided()
        kvw.sided()
        kvw.serve_all()

    @pl.when(jnp.logical_not(direct_line))
    def _():
        wq[0].sided()
        wq[1].sided()
        wq[2].sided()
        wq[3].sided()
        kvw.sided()
        wq[0].serve(1)
        wq[1].serve(1)
        wq[2].serve(1)
        wq[3].serve(1)
        kvw.serve_all()

    arrived(meta_wait)
    wq[0].serve(2)
    wq[1].serve(2)
    metas.start()
    wq[2].serve(2)
    wq[3].serve(2)
    wo[0].start()
    wo[1].start()
    kvw.cross_all()
    metas.serve_all()

    lane = lax.broadcasted_iota(jnp.int32, (1, lanes), 1)
    sign_row = jnp.where(lane % HEAD < HEAD // 2, -1.0, 1.0)
    square_row = lax.broadcasted_iota(jnp.int32, (cap, cap), 0)
    square_col = lax.broadcasted_iota(jnp.int32, (cap, cap), 1)
    slot = lax.broadcasted_iota(jnp.int32, (1, cap), 1)
    wq[0].cross(1)
    wq[1].cross(1)
    wq[0].serve(3)
    wq[1].serve(3)
    for j in range(2):
        spots = (metas_buf[first_shard + j, 0:1, :] + (first_shard + j) * tokens).astype(jnp.float32)
        spot = jnp.sum(jnp.where(square_row == square_col, spots, 0.0), axis=1, keepdims=True)
        angle = spot * rate_ref[...]
        cos_buf[j * cap : (j + 1) * cap, :] = jnp.cos(angle)
        sin_buf[j * cap : (j + 1) * cap, :] = jnp.sin(angle) * sign_row
    wq[2].cross(1)
    wq[3].cross(1)
    arrived(rows_copy)
    kept = wq_buf.at[0, pl.ds(0, 2 * pieces * rows_each)]
    pltpu.make_async_copy(kept, kept, keep_sem).wait()
    kvw_buf[pl.ds(pl.multiple_of(me * rows_each, rows_each), rows_each)] = kvw_own[0]
    kvw.settle()
    x_all = x_buf[...].reshape(slots, width)
    both = jnp.dot(x_all, kvw_buf[...], preferred_element_type=jnp.float32)
    gain = jnp.concatenate([gain_ref[1:2, :], gain_ref[1:2, :]], axis=1)
    mean = jnp.sum(jnp.where(lane < HEAD, both * both, 0.0), axis=1, keepdims=True) * (1.0 / HEAD)
    key = turn(both * lax.rsqrt(mean + norm_eps) * gain, cos_buf[...], sin_buf[...], lane)
    kv_own[...] = jnp.where(lane < HEAD, key, both).astype(jnp.bfloat16)
    wq[2].serve(3)
    wq[3].serve(3)
    wo[0].sided()
    wo[1].sided()
    kv.start()
    kv_buf[pl.ds(pl.multiple_of(first_shard * cap, slots), slots)] = kv_own[...]

    q_gain = jnp.concatenate([gain_ref[0:1, :], gain_ref[0:1, :]], axis=1) * (1.0 / math.sqrt(HEAD))

    def q_piece(k):
        wq[k].settle()
        lin = jnp.dot(x_buf[...].reshape(slots, width), wq_buf[k], preferred_element_type=jnp.float32)
        for t in range(part // lanes):
            total = lin[:, t * lanes : (t + 1) * lanes]
            squares = total * total
            first = jnp.sum(jnp.where(lane < HEAD, squares, 0.0), axis=1, keepdims=True)
            second = jnp.sum(jnp.where(lane < HEAD, 0.0, squares), axis=1, keepdims=True)
            mean = jnp.where(lane < HEAD, first, second) * (1.0 / HEAD)
            values = total * lax.rsqrt(mean + norm_eps) * q_gain
            values = turn(values, cos_buf[...], sin_buf[...], lane)
            h = 2 * (k * (part // lanes) + t)
            q_buf[h] = jnp.where(lane < HEAD, values, 0.0).astype(jnp.bfloat16)
            q_buf[h + 1] = jnp.where(lane < HEAD, pltpu.roll(values, HEAD, 1), 0.0).astype(jnp.bfloat16)

    wq[0].cross(2)
    wq[1].cross(2)
    wo[2].start()
    wo[3].start()
    wo[2].sided()
    wq[2].cross(2)
    wq[3].cross(2)
    wo[3].sided()
    wq[0].cross(3)
    wq[1].cross(3)
    wo[0].serve(1)
    wq[2].cross(3)
    wq[3].cross(3)
    q_piece(0)
    wo[1].serve(1)
    q_piece(1)
    wo[2].serve(1)
    metas.settle()
    starts, counts = [], []
    start = jnp.zeros((1, cap), jnp.int32)
    own_start = [jnp.zeros((1, cap), jnp.int32) for _ in range(2)]
    for s in range(n):
        count = metas_buf[s, 1:2, :]
        starts.append(start)
        counts.append(count)
        start = start + count
        for j in range(2):
            own_start[j] = own_start[j] + jnp.where(first_shard + j > s, count, 0)
    for j in range(2):
        for k in range(keep // cap):
            seen = square_col + k * cap - square_row <= own_start[j]
            mask_buf[j * cap : (j + 1) * cap, k * cap : (k + 1) * cap] = jnp.where(seen, 0.0, -1e30)

    q_piece(2)
    wo[3].serve(1)
    q_piece(3)
    kv.serve_all()
    kv.settle()
    blocks = keep // cap
    for k in range(blocks):
        begin, end = k, min(n, k + n - blocks + 1)
        hits = []
        for s in range(begin, end):
            ranks = jnp.where(slot < counts[s], starts[s] + slot, -1)
            hits.append((square_row + k * cap == ranks).astype(jnp.float32).astype(jnp.bfloat16))
        dense = jnp.dot(jnp.concatenate(hits, axis=1), kv_buf[begin * cap : end * cap, :], preferred_element_type=jnp.float32)
        pairs_buf[k * cap : (k + 1) * cap, :] = dense.astype(jnp.bfloat16)

    def attend_head(h):
        scores = lax.dot_general(
            q_buf[h], pairs_buf[...], (((1,), (1,)), ((), ())), preferred_element_type=jnp.float32
        ) + mask_buf[...]
        top = jnp.max(scores, axis=-1, keepdims=True)
        weights = jnp.exp(scores - top)
        denominator = jnp.sum(weights, axis=-1, keepdims=True)
        mix = jnp.dot(weights.astype(jnp.bfloat16), pairs_buf[...], preferred_element_type=jnp.float32)
        return mix / denominator

    groups = chips // 2

    def att_copy(i, source):
        at = att_buf.at[source * groups + i]
        return remote(at, at, att_send, att_recv, {"blk": p.across + core})

    heads = half // HEAD
    chunk_heads = heads // groups

    def attend_pair(t):
        mixes = [attend_head(2 * t + e) for e in range(2)]
        joined = jnp.where(lane < HEAD, pltpu.roll(mixes[0], HEAD, 1), mixes[1])
        per = chunk_heads // 2
        i, at = t // per, t % per * lanes
        att_buf[y * groups + i, :, at : at + lanes] = joined.astype(jnp.bfloat16)
        if t % per == per - 1:
            att_copy(i, y).start()

    attend_pair(0)
    attend_pair(1)
    wo[0].serve(2)
    attend_pair(2)
    wo[0].cross(1)
    wo[1].serve(2)
    attend_pair(3)
    wo[1].cross(1)
    attend_pair(4)
    wo[2].serve(2)
    attend_pair(5)
    wo[2].cross(1)
    wo[3].serve(2)
    attend_pair(6)
    wo[3].cross(1)
    wo[0].serve(3)
    attend_pair(7)
    wo[1].serve(3)
    wo[0].cross(2)
    wo[2].serve(3)
    wo[1].cross(2)
    wo[3].serve(3)
    wo[0].cross(3)
    wo[1].cross(3)
    for item in [kvw] + wq:
        item.drain()
    whole = att_buf.at[pl.ds(0, groups)]
    remote(whole, whole, att_send, att_recv, {"blk": p.across + core}).wait_recv()

    def out_copy(k, j, here):
        return remote(out_buf.at[k, j], update_buf.at[y, k], out_send, out_recv.at[y, k],
                      {"blk": chip * 2 + j if here else p.across + j})

    for k in range(pieces):
        if k == pieces // 2:
            for late in wo[k:]:
                late.cross(2)
                late.cross(3)
        wo[k].settle()
        total = None
        for i in range(chips):
            product = jnp.dot(att_buf[i], wo_buf[k, i * 2 * rows_each : (i + 1) * 2 * rows_each, :], preferred_element_type=jnp.float32)
            total = product if total is None else total + product
        out_buf[k] = total.astype(jnp.bfloat16).reshape(2, cap, part)

        @pl.when(home_here)
        def _():
            update_buf[y, k] = out_buf[k, core]
            out_copy(k, 1 - core, True).start()

        @pl.when(away)
        def _():
            for j in range(2):
                out_copy(k, j, False).start()

    rows = final_ref[...].astype(jnp.float32)
    gate = jax.nn.sigmoid(jnp.sum(rows * router_ref[...].astype(jnp.float32).reshape(1, width), axis=1, keepdims=True))

    at_slot = lax.broadcasted_iota(jnp.int32, (tokens, cap), 0) == jnp.where(slot < count_ref[...], idx_ref[...], -1)
    put = at_slot.astype(jnp.float32)
    touched = jnp.max(put, axis=1, keepdims=True) > 0.0
    put = put.astype(jnp.bfloat16)

    def placed_copy(h, k):
        cols = slice(h * half + k * part, h * half + (k + 1) * part)
        return pltpu.make_async_copy(placed_buf.at[:, cols], out_ref.at[:, cols], placed_sem.at[h, k])

    def update_wait(h, k):
        remote(out_buf.at[k, 0], update_buf.at[h, k], out_send, out_recv.at[h, k], {"blk": p.across}).wait_recv()

    for k in range(pieces):
        update_wait(1 - y, k)

        @pl.when(away)
        def _():
            update_wait(y, k)

        for h in range(2):
            cols = slice(h * half + k * part, h * half + (k + 1) * part)
            done = (rows[:, cols] + gate * update_buf[h, k].astype(jnp.float32)).astype(jnp.bfloat16)
            placed = jnp.dot(put, done, preferred_element_type=jnp.float32)
            old = hidden_buf[:, cols].astype(jnp.float32)
            placed_buf[:, cols] = jnp.where(touched, placed, old).astype(jnp.bfloat16)
            placed_copy(h, k).start()

    for item in [kv, metas] + wo:
        item.drain()
    remote(whole, whole, att_send, att_recv, {"blk": p.across + core}).wait_send()
    rows_copy(1, core).wait_send()
    meta_copy(1, core).wait_send()

    def out_sent(homes):
        some = out_buf.at[:, pl.ds(0, homes)]
        remote(some, some, out_send, out_recv.at[0, 0], {"blk": p.across}).wait_send()

    @pl.when(home_here)
    def _():
        out_sent(1)

    @pl.when(away)
    def _():
        rows_copy(0, core).wait_send()
        meta_copy(0, core).wait_send()
        out_sent(2)

    for k in range(pieces):
        for h in range(2):
            placed_copy(h, k).wait()


def layer(n, keep, hidden, kept_idx, kept_count, router, norm_gain, qk_gain, query_weight, key_weight,
          value_weight, out_weight):
    tokens, width = hidden.shape
    cap = kept_idx.shape[1]
    pieces = 4
    lanes, chips, depth = 2 * HEAD, n // 2, n // 4
    half, slots = width // 2, 2 * cap
    part = half // pieces
    rows_each = query_weight.shape[0]
    half_size = HEAD // 2
    rates = rope_base ** (-(np.arange(half_size) * 2.0 / HEAD))
    rates = np.tile(rates, lanes // half_size)[None, :].astype(np.float32)
    dma = pltpu.SemaphoreType.DMA
    small = [
        kept_idx, kept_count.reshape(1, 1), norm_gain.reshape(1, width), router, key_weight, value_weight, qk_gain,
        jnp.asarray(rates),
    ]
    return pl.pallas_call(
        functools.partial(layer_kernel, n, pieces),
        out_shape=jax.ShapeDtypeStruct((tokens, width), jnp.bfloat16),
        in_specs=[HBM] * 11,
        out_specs=ANY,
        scratch_shapes=[pltpu.VMEM(a.shape, a.dtype) for a in small]
        + [
            dma((len(small),)),
            pltpu.VMEM((cap, width), jnp.bfloat16),
            pltpu.VMEM((tokens, width), jnp.bfloat16),
            dma((2, pieces)),
            pltpu.VMEM((cap, width), jnp.bfloat16),
            pltpu.VMEM((8, cap), jnp.int32),
            pltpu.VMEM((n, 8, cap), jnp.int32),
            pltpu.VMEM((2, cap, width), jnp.bfloat16),
            pltpu.VMEM((2, rows_each, lanes), jnp.bfloat16),
            pltpu.VMEM((width, lanes), jnp.bfloat16),
            pltpu.VMEM((pieces, width, part), jnp.bfloat16),
            pltpu.VMEM((pieces, width, part), jnp.bfloat16),
            pltpu.VMEM((half // HEAD, slots, lanes), jnp.bfloat16),
            pltpu.VMEM((slots, lanes), jnp.bfloat16),
            pltpu.VMEM((n * cap, lanes), jnp.bfloat16),
            pltpu.VMEM((keep, lanes), jnp.bfloat16),
            pltpu.VMEM((slots, keep), jnp.float32),
            pltpu.VMEM((chips, slots, width // chips), jnp.bfloat16),
            pltpu.VMEM((pieces, 2, cap, part), jnp.bfloat16),
            pltpu.VMEM((2, pieces, cap, part), jnp.bfloat16),
            pltpu.VMEM((slots, lanes), jnp.float32),
            pltpu.VMEM((slots, lanes), jnp.float32),
            dma((2,)), dma((2,)), dma((2,)), dma((2,)),
            dma(()), dma(()), dma(()), dma((2, pieces)),
            dma(()), dma(()), pltpu.VMEM((tokens, width), jnp.bfloat16),
        ]
        + Weight.semaphores(depth, 1 + 2 * pieces)
        + Line.semaphores(depth, 2),
        compiler_params=pltpu.CompilerParams(collective_id=1, has_side_effects=True),
    )(hidden, query_weight, out_weight, *small)


def body(
    n,
    hidden,
    kept_idx,
    kept_count,
    router,
    norm_gain,
    qk_gain,
    query_weight,
    key_weight,
    value_weight,
    out_weight,
):
    tokens = hidden.shape[0]
    cap = kept_idx.shape[1]
    keep = n * (tokens * KEEP_DEV // TOK_DEV)
    return layer(
        n, keep, hidden, kept_idx, kept_count, router, norm_gain, qk_gain, query_weight, key_weight,
        value_weight, out_weight,
    )


def attend(query_heads, query_ranks, key_block, value_block, key_ranks, state):
    prev_top, prev_total, prev_acc = state
    length = key_block.shape[0]
    keys_split = key_block.reshape(length, KV_HEADS, HEAD)
    values_split = value_block.reshape(length, KV_HEADS, HEAD)
    scores = jnp.einsum(
        "agch,bgh->gcab", query_heads, keys_split, preferred_element_type=jnp.float32
    ) * (1.0 / math.sqrt(HEAD))
    allowed = key_ranks[None, :] <= query_ranks[:, None]
    masked = jnp.where(allowed, scores, -1e30)
    new_top = jnp.maximum(prev_top, jnp.max(masked, axis=-1))
    weights = jnp.where(allowed, jnp.exp(masked - new_top[..., None]), 0.0)
    factor = jnp.exp(prev_top - new_top)
    new_total = prev_total * factor + jnp.sum(weights, axis=-1)
    new_acc = prev_acc * factor[..., None] + jnp.einsum(
        "gcab,bgh->gcah",
        weights.astype(jnp.bfloat16),
        values_split,
        preferred_element_type=jnp.float32,
    )
    return (new_top, new_total, new_acc)


def make_fold(query_heads, query_ranks, rank_of, state, pieces):
    key_piece, value_piece = pieces
    length = key_piece.shape[0]

    def inner(block_turn, inner_state):
        block_start = block_turn * 512
        key_block = lax.dynamic_slice_in_dim(key_piece, block_start, 512, 0)
        value_block = lax.dynamic_slice_in_dim(value_piece, block_start, 512, 0)
        key_ranks = rank_of(block_start + jnp.arange(512, dtype=jnp.int32))
        return attend(query_heads, query_ranks, key_block, value_block, key_ranks, inner_state)

    return lax.fori_loop(0, length // 512, inner, state)


def wide_body(
    hidden,
    kept_idx,
    kept_count,
    router,
    norm_gain,
    qk_gain,
    query_weight,
    key_weight,
    value_weight,
    out_weight,
):
    shard_count = lax.axis_size("blk")
    device = lax.axis_index("blk")
    width = hidden.shape[1]
    all_lists, all_counts = (
        lax.all_gather(kept_idx, "blk", axis=0, tiled=True),
        lax.all_gather(kept_count, "blk", axis=0, tiled=True),
    )
    starts = jnp.cumsum(all_counts) - all_counts
    own_start = starts[device]
    own_count = all_counts[device]
    list_slots = jnp.arange(CAP, dtype=jnp.int32)
    is_valid = list_slots < own_count
    token_rows = hidden[kept_idx[0]]
    gate_value = jax.nn.sigmoid(jnp.dot(token_rows, router, preferred_element_type=jnp.float32))
    slot_count = (CAP + shard_count - 1) // shard_count
    outgoing = jnp.where(is_valid[:, None], token_rows, jnp.zeros_like(token_rows))
    outgoing = jnp.roll(outgoing.reshape(slot_count, shard_count, width), own_start, axis=1)
    incoming = lax.all_to_all(outgoing, "blk", split_axis=1, concat_axis=1, tiled=True)
    query_ranks = device + jnp.arange(KEEP_DEV, dtype=jnp.int32) * shard_count
    source_ends = starts + all_counts
    source = jnp.sum((source_ends[None, :] <= query_ranks[:, None]).astype(jnp.int32), axis=1)
    within = query_ranks - starts[source]
    flat_index = within // shard_count * shard_count + source
    kept_rows = incoming.reshape(slot_count * shard_count, width)[flat_index]
    positions = source * TOK_DEV + all_lists[source, within]
    row_total = kept_rows.shape[0]
    normed = rms_scale(kept_rows.astype(jnp.float32), norm_gain).astype(jnp.bfloat16)
    query_cols = Q_HEADS * HEAD
    kv_cols = KV_HEADS * HEAD
    full_query, full_key, full_value, full_out = (
        lax.all_gather(query_weight, "blk", axis=0, tiled=True),
        lax.all_gather(key_weight, "blk", axis=0, tiled=True),
        lax.all_gather(value_weight, "blk", axis=0, tiled=True),
        lax.all_gather(out_weight, "blk", axis=0, tiled=True),
    )
    query_lin = jnp.dot(normed, full_query, preferred_element_type=jnp.float32)
    key_lin = jnp.dot(normed, full_key, preferred_element_type=jnp.float32)
    value_lin = jnp.dot(normed, full_value, preferred_element_type=jnp.float32)
    half_size = HEAD // 2
    rotation_rates = rope_base ** (-(jnp.arange(half_size, dtype=jnp.float32) * 2.0 / HEAD))
    angles = (positions.astype(jnp.float32)[:, None] * rotation_rates[None, :])[:, None, :]
    query_heads = rotate(
        rms_scale(query_lin.reshape(row_total, Q_HEADS, HEAD), qk_gain[0]), angles
    ).astype(jnp.bfloat16)
    key_heads = rotate(
        rms_scale(key_lin.reshape(row_total, KV_HEADS, HEAD), qk_gain[1]), angles
    ).astype(jnp.bfloat16)
    query_heads = query_heads.reshape(row_total, KV_HEADS, Q_HEADS // KV_HEADS, HEAD)
    key_flat = key_heads.reshape(row_total, kv_cols)
    value_flat = value_lin.astype(jnp.bfloat16)
    group_size = Q_HEADS // KV_HEADS
    start_state = (
        jnp.full((KV_HEADS, group_size, row_total), -1e30, jnp.float32),
        jnp.zeros((KV_HEADS, group_size, row_total), jnp.float32),
        jnp.zeros((KV_HEADS, group_size, row_total, HEAD), jnp.float32),
    )

    def strided_rank(slots_seen):
        return slots_seen // KEEP_DEV + slots_seen % KEEP_DEV * shard_count

    final_top, final_total, final_acc = make_fold(
        query_heads,
        query_ranks,
        strided_rank,
        start_state,
        (
            lax.all_gather(key_flat, "blk", axis=0, tiled=True),
            lax.all_gather(value_flat, "blk", axis=0, tiled=True),
        ),
    )
    attended = (
        (final_acc / final_total[..., None])
        .transpose(2, 0, 1, 3)
        .reshape(row_total, query_cols)
        .astype(jnp.bfloat16)
    )
    update = jnp.dot(attended, full_out, preferred_element_type=jnp.float32)
    update = update.astype(jnp.bfloat16)
    slot_grid = (
        jnp.arange(slot_count, dtype=jnp.int32)[:, None] * shard_count
        + jnp.mod(device - starts, shard_count)[None, :]
    )
    back_valid = slot_grid < all_counts[None, :]
    local_place = (starts[None, :] + slot_grid - device) // shard_count
    clipped = jnp.where(back_valid, local_place, 0)
    back_rows = jnp.where(back_valid[..., None], update[clipped], jnp.zeros((), jnp.bfloat16))
    returned = lax.all_to_all(back_rows, "blk", split_axis=1, concat_axis=1, tiled=True)
    returned = jnp.roll(returned, -own_start, axis=1).reshape(slot_count * shard_count, width)
    final = (
        token_rows.astype(jnp.float32) + gate_value[:, None] * returned.astype(jnp.float32)
    ).astype(jnp.bfloat16)
    target = jnp.where(is_valid, kept_idx[0], TOK_DEV)
    return hidden.at[target].set(final, mode="drop")


def solution(mesh):
    placed = (
        P(("groups", "blk"), None),
        P(("groups", "blk"), None),
        P(("groups", "blk")),
        P(),
        P(),
        P(),
        P("blk", None),
        P("blk", None),
        P("blk", None),
        P("blk", None),
    )
    n = mesh.shape["blk"]
    by_heads = n % 4 == 0 and Q_HEADS == 2 * n and mesh.shape["groups"] == KV_HEADS
    step = functools.partial(body, n) if by_heads else wide_body
    return jax.shard_map(
        step, mesh=mesh, in_specs=placed, out_specs=P(("groups", "blk"), None), check_vma=False
    )
```

time: 91.5 us -> 73.9 us (0.81)
  Pallas kernels: 85.3 us -> 69.9 us
  matrix products: 3.07 us -> 0 us
  local copies, waits for them, and re-layouts: 1.31 us -> 3.16 us
    pallas_call x1, Pallas kernels: 85.3 us -> 69.9 us  [layer(): pl.pallas_call(functools.partial(layer_kernel, n, pieces), out_shape=jax....]
    unnamed x4 -> x1, local copies, waits for them, and re-layouts: 0.01 us -> 3.16 us
    dot_general x1 -> x0, matrix products: 3.07 us -> none  [body(): jnp.dot(put.astype(jnp.bfloat16), final, preferred_element_type=jnp.float32)]
    reshape x1 -> x0, local copies, waits for them, and re-layouts: 1.3 us -> none  [layer(): router.reshape(1, width)]
where the time goes in v2:
time: 73.9 us; the launch traced here: 73.8 us
  Pallas kernels  69.9 us (95%)
  local copies, waits for them, and re-layouts  3.16 us (4%)
    pallas_call x1, Pallas kernels, layer(): pl.pallas_call(functools.partial(layer_kernel, n, pieces), out_shape=jax....  69.9 us
    unnamed x1, local copies, waits for them, and re-layouts  3.16 us

profile of v2, /device:TPU:1, one launch (start us, length us, event | category | flops | bytes accessed | tf_op | source)
XLA Modules:
  0.0 73.8 jit_solution(11317785515264596439)
XLA Ops:
  0.7 69.9 %shard_map.109 = bf16[512,2048]{1,0:T(8,128)(2,1)} custom-call(bf16[512,2048]{1,0:T(8,128)(2,1)} %hidden_ref.1, bf16[128,2048]{1,0:T(8,128)(2,1)} %wq_ref.1, bf16[128,2048]{1,0:T(8,128)(2,1)} %wo_ref.1, s32[1,128]{1,0:T(1,128)} %idx_hbm.1, s32[1,1]{1,0:T(1,128)} %bitcast.2.count_hbm, f32[1,2048]{1,0:T(1,128)} %bitcast.3, bf16[2048]{0:T(1024)(128)(2,1)} %router_hbm.1, ...), custom_call_target="tpu_custom_call" | custom-call | tf_op jit(solution)/shard_map/pallas_call | solution.py:655
  70.6 3.2 %copy.14 = bf16[512,2048]{1,0:T(8,128)(2,1)} copy(bf16[512,2048]{1,0:T(8,128)(2,1)} %shard_map.109) | data formatting | bytes 4194304

commit v3 on v2

--- a/solution.py
+++ b/solution.py
@@ -144,83 +144,126 @@
         self.dup(whole, whole).wait_send()
 
 
-class Weight(Line):
-    def __init__(self, place, mine, theirs, buf, sems, direct=False):
-        self.place, self.mine, self.theirs, self.buf, self.direct = place, mine, theirs, buf, direct
-        self.rows = mine.shape[0]
-        self.z_send, self.z_recv, self.dup_send, self.dup_recv = sems[:4]
-        self.side_recv, self.side_send, self.x_recv = sems[4:]
-        self.dups = 2 * place.depth
+class Shared:
+    def __init__(self, place, ref, buf, sems):
+        self.place, self.ref, self.buf = place, ref, buf
+        self.pieces, self.part = buf.shape[0], buf.shape[2]
+        self.rows, self.half = ref.shape[0], self.pieces * buf.shape[2]
+        self.per = self.pieces // 2
+        self.z_send, self.z_recv, self.x_recv, self.side_send, self.side_recv, self.dup_send, self.dup_recv = sems
 
     @staticmethod
-    def semaphores(depth, count):
+    def semaphores(depth, pieces, count):
         dma = pltpu.SemaphoreType.DMA
-        return Line.semaphores(depth, count) + [dma((count,)), dma((count,)), dma((count, depth))]
-
-    def block(self, z, y, core):
+        return [dma((count,)), dma((count, pieces, depth)), dma((count, pieces, depth)), dma((count,)),
+                dma((count, pieces)), dma((count,)), dma((count, pieces))]
+
+    def columns(self, of, k):
+        at = of * self.half + k * self.part
+        return self.ref.at[:, pl.ds(pl.multiple_of(at, self.part), self.part)]
+
+    def block(self, k, z, y, core):
         at = (4 * z + 2 * y + core) * self.rows
-        return self.buf.at[pl.ds(pl.multiple_of(at, self.rows), self.rows)]
-
-    def view(self, z, core):
-        return self.block(z, self.place.group, core)
-
-    def side(self, y):
-        p = self.place
-        return remote(self.theirs, self.block(p.z, y, p.core), self.side_send, self.side_recv, {"blk": p.across + p.core})
-
-    def other(self, z, group):
-        block = self.block(z, group, self.place.core)
-        return remote(block, block, self.side_send, self.x_recv.at[z], {"groups": 1 - self.place.group})
-
-    def start_side(self):
-        self.side(self.place.y).start()
+        return self.buf.at[k, pl.ds(pl.multiple_of(at, self.rows), self.rows)]
+
+    def piece(self, unit, group):
+        return self.per * group + unit % self.per
+
+    def unit(self, unit, z, group):
+        p = self.place
+        return self.block(self.piece(unit, group), z, p.y if unit < self.per else 1 - p.y, p.core)
+
+    def dup(self, k, source, target):
+        return remote(source, target, self.dup_send, self.dup_recv.at[k], {"blk": self.place.partner})
+
+    def side(self, k, y):
+        p = self.place
+        return remote(self.columns(1 - p.y, k), self.block(k, p.z, y, p.core), self.side_send, self.side_recv.at[k],
+                      {"blk": p.across + p.core})
+
+    def along(self, unit, source, z, sign):
+        p = self.place
+        return remote(source, self.unit(unit, z, p.group), self.z_send, self.z_recv.at[unit, z], {"blk": p.me + 4 * sign})
+
+    def other(self, unit, z, group):
+        block = self.unit(unit, z, group)
+        return remote(block, block, self.side_send, self.x_recv.at[unit, z], {"groups": 1 - self.place.group})
+
+    def start_side(self, group):
+        for unit in range(self.per):
+            self.side(self.piece(unit, group), self.place.y).start()
+
+    def launch(self, unit, source):
+        p = self.place
+        for sign in (1, -1):
+            @pl.when(p.inside(p.z + sign))
+            def _():
+                self.along(unit, source, p.z, sign).start()
 
     def start(self):
         p = self.place
-
-        @pl.when(p.y == p.group)
-        def _():
-            self.launch(self.mine)
-
-        self.dup(self.mine, self.block(p.z, p.y, p.core)).start()
-
-    def keep(self, sem):
-        p = self.place
-        return pltpu.make_async_copy(self.mine, self.block(p.z, p.y, p.core), sem)
-
-    def sided(self):
-        p = self.place
-        block = self.block(p.z, 1 - p.y, p.core)
-        self.side(1 - p.y).wait_recv()
-
-        @pl.when(p.y != p.group)
-        def _():
-            self.launch(block)
-
-        self.dup(block, block).start()
-
-    def passed(self, z):
-        self.other(z, self.place.group).start()
-
-    def cross(self, distance):
+        for unit in range(self.per):
+            self.launch(unit, self.columns(p.y, self.piece(unit, p.group)))
+        for k in range(self.pieces):
+            self.dup(k, self.columns(p.y, k), self.block(k, p.z, p.y, p.core)).start()
+
+    def keep(self, k, sem):
+        p = self.place
+        return pltpu.make_async_copy(self.columns(p.y, k), self.block(k, p.z, p.y, p.core), sem)
+
+    def sided(self, unit, carried=True):
+        p = self.place
+        k = self.piece(unit, p.group if carried else 1 - p.group)
+        block = self.block(k, p.z, 1 - p.y, p.core)
+        self.side(k, 1 - p.y).wait_recv()
+        if carried:
+            self.launch(self.per + unit, block)
+        self.dup(k, block, block).start()
+
+    def serve(self, unit, distance):
         p = self.place
         for sign in (1, -1):
             z = p.z - sign * distance
 
             @pl.when(p.inside(z))
             def _():
-                self.other(z, 1 - p.group).wait_recv()
-                block = self.block(z, 1 - p.group, p.core)
-                self.dup(block, block).start()
-
-    def cross_all(self):
-        for distance in range(1, self.place.depth):
-            self.cross(distance)
+                block = self.unit(unit, z, p.group)
+                self.along(unit, block, z, sign).wait_recv()
+
+                @pl.when(p.inside(p.z + sign))
+                def _():
+                    self.along(unit, block, z, sign).start()
+
+                self.other(unit, z, p.group).start()
+                self.dup(self.piece(unit, p.group), block, block).start()
+
+    def cross(self, unit, distance):
+        p = self.place
+        for sign in (1, -1):
+            z = p.z - sign * distance
+
+            @pl.when(p.inside(z))
+            def _():
+                self.other(unit, z, 1 - p.group).wait_recv()
+                block = self.unit(unit, z, 1 - p.group)
+                self.dup(self.piece(unit, 1 - p.group), block, block).start()
+
+    def settle(self, k):
+        whole = self.buf.at[k, pl.ds(0, 2 * self.place.depth * self.rows)]
+        self.dup(k, whole, whole).wait_recv()
 
     def drain(self):
-        super().drain()
-        whole = self.total(self.place.depth)
-        remote(whole, whole, self.side_send, self.side_recv, {"blk": self.place.partner}).wait_send()
+        p = self.place
+
+        def sent(sem, blocks):
+            whole = self.buf.at[:, pl.ds(0, blocks * self.rows)]
+            remote(whole, whole, sem, self.side_recv.at[0], {"blk": p.partner}).wait_send()
+
+        middle = jnp.logical_and(p.z > 0, p.z < p.depth - 1)
+        pl.when(middle)(lambda: sent(self.z_send, p.depth + 1))
+        pl.when(jnp.logical_not(middle))(lambda: sent(self.z_send, 1))
+        sent(self.side_send, p.depth)
+        sent(self.dup_send, 2 * p.depth)
 
 
 def turn(values, cosine, sine, lane):
@@ -252,8 +295,6 @@
         (gain_hbm, gain_ref), (rate_hbm, rate_ref), (router_hbm, router_ref)))]
     for copy in small:
         copy.start()
-    for item in small:
-        item.wait()
     tokens, width = hidden_ref.shape
     cap = idx_ref.shape[1]
     lanes = 2 * HEAD
@@ -265,28 +306,24 @@
     away = jnp.logical_not(home_here)
     first_shard = 4 * p.z + 2 * core
 
-    def head_side(ref, of):
-        return jnp.where(of == 0, ref[:, :HEAD].astype(jnp.float32), ref[:, HEAD:].astype(jnp.float32))
-
-    for k, of in enumerate((y, 1 - y)):
-        kvw_own[k] = jnp.concatenate([head_side(wk_ref, of), head_side(wv_ref, of)], axis=1).astype(jnp.bfloat16)
-    line = lax.broadcasted_iota(jnp.int32, meta_buf.shape, 0)
-    meta_buf[...] = jnp.where(line == 0, idx_ref[...], count_ref[...])
-
-    def columns(ref, of, k):
-        return ref.at[:, pl.ds(pl.multiple_of(of * half + k * part, part), part)]
-
     rows_each = wq_ref.shape[0]
 
     def take(sems, i):
         return [s.at[i] for s in sems]
 
-    w_sems, a_sems = sems[:7], sems[7:]
-    kvw = Weight(p, kvw_own.at[0], kvw_own.at[1], kvw_buf, take(w_sems, 0), direct=True)
-    wq = [Weight(p, columns(wq_ref, y, k), columns(wq_ref, 1 - y, k), wq_buf.at[k], take(w_sems, 1 + k))
-          for k in range(pieces)]
-    wo = [Weight(p, columns(wo_ref, y, k), columns(wo_ref, 1 - y, k), wo_buf.at[k], take(w_sems, 1 + pieces + k))
-          for k in range(pieces)]
+    kvw_sems, a_sems, s_sems = sems[0], sems[1:5], sems[5:]
+    def kvw_view(of):
+        def view(z, at_core):
+            at = (4 * z + 2 * of + at_core) * rows_each
+            return kvw_buf.at[pl.ds(pl.multiple_of(at, rows_each), rows_each)]
+        return view
+
+    kvw_sources = (kvw_own.at[0], kvw_view(1 - y)(p.z, core))
+    kvw_lines = [Line(p, source, kvw_buf, rows_each, kvw_view(of), take(a_sems, 2 + k))
+                 for k, (source, of) in enumerate(zip(kvw_sources, (y, 1 - y)))]
+    kvw_cross = remote(kvw_own.at[1], kvw_view(y)(p.z, core), kvw_sems.at[0], kvw_sems.at[1], {"blk": p.across + core})
+    wq = Shared(p, wq_ref, wq_buf, take(s_sems, 0))
+    wo = Shared(p, wo_ref, wo_buf, take(s_sems, 1))
 
     def pair_of(buf, each):
         def view(z, of):
@@ -318,14 +355,24 @@
             def _():
                 copy(1, j).wait_recv()
 
-    for item in wq + wo:
-        item.keep(keep_sem).start()
+    for item in (wq, wo):
+        for k in range(pieces):
+            item.keep(k, keep_sem).start()
     pl.semaphore_wait(barrier, 4 + depth - 1)
-    first = wq + [kvw]
-    for item in first:
-        item.start_side()
-    for item in first:
-        item.start()
+    wq.start_side(p.group)
+    wq.start()
+    for item in small:
+        item.wait()
+    def head_side(ref, of):
+        return jnp.where(of == 0, ref[:, :HEAD].astype(jnp.float32), ref[:, HEAD:].astype(jnp.float32))
+
+    for k, of in enumerate((y, 1 - y)):
+        kvw_own[k] = jnp.concatenate([head_side(wk_ref, of), head_side(wv_ref, of)], axis=1).astype(jnp.bfloat16)
+    line = lax.broadcasted_iota(jnp.int32, meta_buf.shape, 0)
+    meta_buf[...] = jnp.where(line == 0, idx_ref[...], count_ref[...])
+
+    kvw_cross.start()
+    kvw_lines[0].start()
     meta_copy(1, core).start()
 
     @pl.when(home_here)
@@ -356,86 +403,64 @@
     def _():
         rows_copy(0, core).start()
 
-    for item in wo:
-        item.start_side()
-    direct_line = y == p.group
-
-    @pl.when(direct_line)
-    def _():
-        wq[0].serve(1)
-        wq[1].serve(1)
-        wq[0].sided()
-        wq[2].serve(1)
-        wq[1].sided()
-        wq[3].serve(1)
-        wq[2].sided()
-        wq[3].sided()
-        kvw.sided()
-        kvw.serve_all()
-
-    @pl.when(jnp.logical_not(direct_line))
-    def _():
-        wq[0].sided()
-        wq[1].sided()
-        wq[2].sided()
-        wq[3].sided()
-        kvw.sided()
-        wq[0].serve(1)
-        wq[1].serve(1)
-        wq[2].serve(1)
-        wq[3].serve(1)
-        kvw.serve_all()
-
+    wo.start_side(p.group)
+    wq.start_side(1 - p.group)
+    wo.start_side(1 - p.group)
+    wq.sided(0)
+    wq.serve(0, 1)
+    wq.sided(1)
+    kvw_cross.wait_recv()
+    kvw_lines[1].start()
+    wq.serve(1, 1)
+    wq.serve(2, 1)
+    wq.serve(0, 2)
+    wq.serve(3, 1)
+    wq.serve(1, 2)
     arrived(meta_wait)
-    wq[0].serve(2)
-    wq[1].serve(2)
     metas.start()
-    wq[2].serve(2)
-    wq[3].serve(2)
-    wo[0].start()
-    wo[1].start()
-    kvw.cross_all()
-    metas.serve_all()
+    wq.serve(2, 2)
+    wq.cross(0, 1)
+    wq.serve(0, 3)
+    wq.cross(1, 1)
+    wq.serve(3, 2)
+    wq.cross(2, 1)
+    wq.cross(0, 2)
+    wo.start()
 
     lane = lax.broadcasted_iota(jnp.int32, (1, lanes), 1)
     sign_row = jnp.where(lane % HEAD < HEAD // 2, -1.0, 1.0)
     square_row = lax.broadcasted_iota(jnp.int32, (cap, cap), 0)
     square_col = lax.broadcasted_iota(jnp.int32, (cap, cap), 1)
     slot = lax.broadcasted_iota(jnp.int32, (1, cap), 1)
-    wq[0].cross(1)
-    wq[1].cross(1)
-    wq[0].serve(3)
-    wq[1].serve(3)
     for j in range(2):
         spots = (metas_buf[first_shard + j, 0:1, :] + (first_shard + j) * tokens).astype(jnp.float32)
         spot = jnp.sum(jnp.where(square_row == square_col, spots, 0.0), axis=1, keepdims=True)
         angle = spot * rate_ref[...]
         cos_buf[j * cap : (j + 1) * cap, :] = jnp.cos(angle)
         sin_buf[j * cap : (j + 1) * cap, :] = jnp.sin(angle) * sign_row
-    wq[2].cross(1)
-    wq[3].cross(1)
+    wq.cross(3, 1)
+    metas.serve_all()
+    for item in kvw_lines:
+        item.serve_all()
     arrived(rows_copy)
     kept = wq_buf.at[0, pl.ds(0, 2 * pieces * rows_each)]
     pltpu.make_async_copy(kept, kept, keep_sem).wait()
     kvw_buf[pl.ds(pl.multiple_of(me * rows_each, rows_each), rows_each)] = kvw_own[0]
-    kvw.settle()
+    for item in kvw_lines:
+        item.settle()
     x_all = x_buf[...].reshape(slots, width)
     both = jnp.dot(x_all, kvw_buf[...], preferred_element_type=jnp.float32)
     gain = jnp.concatenate([gain_ref[1:2, :], gain_ref[1:2, :]], axis=1)
     mean = jnp.sum(jnp.where(lane < HEAD, both * both, 0.0), axis=1, keepdims=True) * (1.0 / HEAD)
     key = turn(both * lax.rsqrt(mean + norm_eps) * gain, cos_buf[...], sin_buf[...], lane)
     kv_own[...] = jnp.where(lane < HEAD, key, both).astype(jnp.bfloat16)
-    wq[2].serve(3)
-    wq[3].serve(3)
-    wo[0].sided()
-    wo[1].sided()
     kv.start()
     kv_buf[pl.ds(pl.multiple_of(first_shard * cap, slots), slots)] = kv_own[...]
 
     q_gain = jnp.concatenate([gain_ref[0:1, :], gain_ref[0:1, :]], axis=1) * (1.0 / math.sqrt(HEAD))
 
     def q_piece(k):
-        wq[k].settle()
+        wq.settle(k)
         lin = jnp.dot(x_buf[...].reshape(slots, width), wq_buf[k], preferred_element_type=jnp.float32)
         for t in range(part // lanes):
             total = lin[:, t * lanes : (t + 1) * lanes]
@@ -449,23 +474,24 @@
             q_buf[h] = jnp.where(lane < HEAD, values, 0.0).astype(jnp.bfloat16)
             q_buf[h + 1] = jnp.where(lane < HEAD, pltpu.roll(values, HEAD, 1), 0.0).astype(jnp.bfloat16)
 
-    wq[0].cross(2)
-    wq[1].cross(2)
-    wo[2].start()
-    wo[3].start()
-    wo[2].sided()
-    wq[2].cross(2)
-    wq[3].cross(2)
-    wo[3].sided()
-    wq[0].cross(3)
-    wq[1].cross(3)
-    wo[0].serve(1)
-    wq[2].cross(3)
-    wq[3].cross(3)
-    q_piece(0)
-    wo[1].serve(1)
-    q_piece(1)
-    wo[2].serve(1)
+    wq.serve(1, 3)
+    wq.serve(2, 3)
+    wq.cross(1, 2)
+    wq.serve(3, 3)
+    wq.cross(2, 2)
+    wo.sided(0)
+    wq.cross(0, 3)
+    wo.sided(1)
+    wq.cross(3, 2)
+    q_piece(wq.piece(0,p.group))
+    wo.serve(0, 1)
+    wq.cross(1, 3)
+    q_piece(wq.piece(1,p.group))
+    wo.serve(1, 1)
+    wq.sided(0, False)
+    wq.sided(1, False)
+    wq.cross(2, 3)
+    wq.cross(3, 3)
     metas.settle()
     starts, counts = [], []
     start = jnp.zeros((1, cap), jnp.int32)
@@ -482,10 +508,10 @@
             seen = square_col + k * cap - square_row <= own_start[j]
             mask_buf[j * cap : (j + 1) * cap, k * cap : (k + 1) * cap] = jnp.where(seen, 0.0, -1e30)
 
-    q_piece(2)
-    wo[3].serve(1)
-    q_piece(3)
+    q_piece(wq.piece(0,1-p.group))
     kv.serve_all()
+    q_piece(wq.piece(1,1-p.group))
+    wo.serve(2, 1)
     kv.settle()
     blocks = keep // cap
     for k in range(blocks):
@@ -509,8 +535,8 @@
 
     groups = chips // 2
 
-    def att_copy(i, source):
-        at = att_buf.at[source * groups + i]
+    def att_copy(i, at, source):
+        at = att_buf.at[source * groups + i, :, pl.ds(at, lanes)]
         return remote(at, at, att_send, att_recv, {"blk": p.across + core})
 
     heads = half // HEAD
@@ -522,34 +548,35 @@
         per = chunk_heads // 2
         i, at = t // per, t % per * lanes
         att_buf[y * groups + i, :, at : at + lanes] = joined.astype(jnp.bfloat16)
-        if t % per == per - 1:
-            att_copy(i, y).start()
+        att_copy(i, at, y).start()
 
     attend_pair(0)
+    wo.serve(3, 1)
+    wo.serve(0, 2)
     attend_pair(1)
-    wo[0].serve(2)
+    wo.serve(2, 2)
     attend_pair(2)
-    wo[0].cross(1)
-    wo[1].serve(2)
+    wo.serve(1, 2)
+    wo.cross(0, 1)
+    wo.sided(0, False)
+    wo.sided(1, False)
     attend_pair(3)
-    wo[1].cross(1)
+    wo.serve(3, 2)
+    wo.cross(1, 1)
     attend_pair(4)
-    wo[2].serve(2)
+    wo.cross(2, 1)
+    wo.serve(0, 3)
     attend_pair(5)
-    wo[2].cross(1)
-    wo[3].serve(2)
+    wo.serve(2, 3)
+    wo.cross(0, 2)
     attend_pair(6)
-    wo[3].cross(1)
-    wo[0].serve(3)
+    wo.serve(1, 3)
+    wo.cross(3, 1)
+    wo.cross(2, 2)
     attend_pair(7)
-    wo[1].serve(3)
-    wo[0].cross(2)
-    wo[2].serve(3)
-    wo[1].cross(2)
-    wo[3].serve(3)
-    wo[0].cross(3)
-    wo[1].cross(3)
-    for item in [kvw] + wq:
+    wo.serve(3, 3)
+    kvw_cross.wait_send()
+    for item in (*kvw_lines, wq):
         item.drain()
     whole = att_buf.at[pl.ds(0, groups)]
     remote(whole, whole, att_send, att_recv, {"blk": p.across + core}).wait_recv()
@@ -558,15 +585,20 @@
         return remote(out_buf.at[k, j], update_buf.at[y, k], out_send, out_recv.at[y, k],
                       {"blk": chip * 2 + j if here else p.across + j})
 
-    for k in range(pieces):
-        if k == pieces // 2:
-            for late in wo[k:]:
-                late.cross(2)
-                late.cross(3)
-        wo[k].settle()
+    order = [wo.piece(unit, group) for group in (p.group, 1 - p.group) for unit in range(pieces // 2)]
+    for i, k in enumerate(order):
+        if i == 1:
+            wo.cross(1, 2)
+            wo.cross(3, 2)
+            wo.cross(0, depth - 1)
+            wo.cross(2, depth - 1)
+        if i == 2:
+            wo.cross(1, depth - 1)
+            wo.cross(3, depth - 1)
+        wo.settle(k)
         total = None
-        for i in range(chips):
-            product = jnp.dot(att_buf[i], wo_buf[k, i * 2 * rows_each : (i + 1) * 2 * rows_each, :], preferred_element_type=jnp.float32)
+        for c in range(chips):
+            product = jnp.dot(att_buf[c], wo_buf[k, c * 2 * rows_each : (c + 1) * 2 * rows_each, :], preferred_element_type=jnp.float32)
             total = product if total is None else total + product
         out_buf[k] = total.astype(jnp.bfloat16).reshape(2, cap, part)
 
@@ -588,14 +620,17 @@
     touched = jnp.max(put, axis=1, keepdims=True) > 0.0
     put = put.astype(jnp.bfloat16)
 
+    def spot_of(h, k):
+        return pl.ds(pl.multiple_of(h * half + k * part, part), part)
+
     def placed_copy(h, k):
-        cols = slice(h * half + k * part, h * half + (k + 1) * part)
+        cols = spot_of(h, k)
         return pltpu.make_async_copy(placed_buf.at[:, cols], out_ref.at[:, cols], placed_sem.at[h, k])
 
     def update_wait(h, k):
         remote(out_buf.at[k, 0], update_buf.at[h, k], out_send, out_recv.at[h, k], {"blk": p.across}).wait_recv()
 
-    for k in range(pieces):
+    for i, k in enumerate(order):
         update_wait(1 - y, k)
 
         @pl.when(away)
@@ -603,14 +638,14 @@
             update_wait(y, k)
 
         for h in range(2):
-            cols = slice(h * half + k * part, h * half + (k + 1) * part)
-            done = (rows[:, cols] + gate * update_buf[h, k].astype(jnp.float32)).astype(jnp.bfloat16)
+            cols = spot_of(h, k)
+            done = (final_ref[:, cols].astype(jnp.float32) + gate * update_buf[h, k].astype(jnp.float32)).astype(jnp.bfloat16)
             placed = jnp.dot(put, done, preferred_element_type=jnp.float32)
             old = hidden_buf[:, cols].astype(jnp.float32)
             placed_buf[:, cols] = jnp.where(touched, placed, old).astype(jnp.bfloat16)
             placed_copy(h, k).start()
 
-    for item in [kv, metas] + wo:
+    for item in (kv, metas, wo):
         item.drain()
     remote(whole, whole, att_send, att_recv, {"blk": p.across + core}).wait_send()
     rows_copy(1, core).wait_send()
@@ -685,8 +720,9 @@
             dma(()), dma(()), dma(()), dma((2, pieces)),
             dma(()), dma(()), pltpu.VMEM((tokens, width), jnp.bfloat16),
         ]
-        + Weight.semaphores(depth, 1 + 2 * pieces)
-        + Line.semaphores(depth, 2),
+        + [dma((2,))]
+        + Line.semaphores(depth, 4)
+        + Shared.semaphores(depth, pieces, 2),
         compiler_params=pltpu.CompilerParams(collective_id=1, has_side_effects=True),
     )(hidden, query_weight, out_weight, *small)
 

time: 73.9 us -> 68.5 us (0.927)
  Pallas kernels: 69.9 us -> 64.5 us
    pallas_call x1, Pallas kernels: 69.9 us -> 64.5 us  [layer(): pl.pallas_call(functools.partial(layer_kernel, n, pieces), out_shape=jax....]
where the time goes in v3:
time: 68.5 us; the launch traced here: 68.3 us
  Pallas kernels  64.5 us (94%)
  local copies, waits for them, and re-layouts  3.16 us (5%)
    pallas_call x1, Pallas kernels, layer(): pl.pallas_call(functools.partial(layer_kernel, n, pieces), out_shape=jax....  64.5 us
    unnamed x1, local copies, waits for them, and re-layouts  3.16 us

profile of v3, /device:TPU:1, one launch (start us, length us, event | category | flops | bytes accessed | tf_op | source)
XLA Modules:
  0.0 68.3 jit_solution(6192978604381957310)
XLA Ops:
  0.7 64.5 %shard_map.109 = bf16[512,2048]{1,0:T(8,128)(2,1)} custom-call(bf16[512,2048]{1,0:T(8,128)(2,1)} %hidden_ref.1, bf16[128,2048]{1,0:T(8,128)(2,1)} %wq_ref.1, bf16[128,2048]{1,0:T(8,128)(2,1)} %wo_ref.1, s32[1,128]{1,0:T(1,128)} %idx_hbm.1, s32[1,1]{1,0:T(1,128)} %bitcast.2.count_hbm, f32[1,2048]{1,0:T(1,128)} %bitcast.3, bf16[2048]{0:T(1024)(128)(2,1)} %router_hbm.1, ...), custom_call_target="tpu_custom_call" | custom-call | tf_op jit(solution)/shard_map/pallas_call | solution.py:690
  65.2 3.2 %copy.14 = bf16[512,2048]{1,0:T(8,128)(2,1)} copy(bf16[512,2048]{1,0:T(8,128)(2,1)} %shard_map.109) | data formatting | bytes 4194304

commit v4 on v3

--- a/solution.py
+++ b/solution.py
@@ -413,18 +413,18 @@
     kvw_lines[1].start()
     wq.serve(1, 1)
     wq.serve(2, 1)
+    arrived(meta_wait)
+    metas.start()
     wq.serve(0, 2)
     wq.serve(3, 1)
     wq.serve(1, 2)
-    arrived(meta_wait)
-    metas.start()
     wq.serve(2, 2)
+    for item in kvw_lines:
+        item.serve_all()
     wq.cross(0, 1)
     wq.serve(0, 3)
     wq.cross(1, 1)
     wq.serve(3, 2)
-    wq.cross(2, 1)
-    wq.cross(0, 2)
     wo.start()
 
     lane = lax.broadcasted_iota(jnp.int32, (1, lanes), 1)
@@ -438,10 +438,6 @@
         angle = spot * rate_ref[...]
         cos_buf[j * cap : (j + 1) * cap, :] = jnp.cos(angle)
         sin_buf[j * cap : (j + 1) * cap, :] = jnp.sin(angle) * sign_row
-    wq.cross(3, 1)
-    metas.serve_all()
-    for item in kvw_lines:
-        item.serve_all()
     arrived(rows_copy)
     kept = wq_buf.at[0, pl.ds(0, 2 * pieces * rows_each)]
     pltpu.make_async_copy(kept, kept, keep_sem).wait()
@@ -475,6 +471,9 @@
             q_buf[h + 1] = jnp.where(lane < HEAD, pltpu.roll(values, HEAD, 1), 0.0).astype(jnp.bfloat16)
 
     wq.serve(1, 3)
+    wq.cross(2, 1)
+    wq.cross(0, 2)
+    wq.cross(3, 1)
     wq.serve(2, 3)
     wq.cross(1, 2)
     wq.serve(3, 3)
@@ -483,11 +482,11 @@
     wq.cross(0, 3)
     wo.sided(1)
     wq.cross(3, 2)
+    metas.serve_all()
     q_piece(wq.piece(0,p.group))
     wo.serve(0, 1)
     wq.cross(1, 3)
     q_piece(wq.piece(1,p.group))
-    wo.serve(1, 1)
     wq.sided(0, False)
     wq.sided(1, False)
     wq.cross(2, 3)
@@ -509,9 +508,9 @@
             mask_buf[j * cap : (j + 1) * cap, k * cap : (k + 1) * cap] = jnp.where(seen, 0.0, -1e30)
 
     q_piece(wq.piece(0,1-p.group))
+    wo.serve(1, 1)
     kv.serve_all()
     q_piece(wq.piece(1,1-p.group))
-    wo.serve(2, 1)
     kv.settle()
     blocks = keep // cap
     for k in range(blocks):
@@ -551,30 +550,31 @@
         att_copy(i, at, y).start()
 
     attend_pair(0)
+    wo.serve(2, 1)
     wo.serve(3, 1)
+    attend_pair(1)
     wo.serve(0, 2)
-    attend_pair(1)
+    attend_pair(2)
+    wo.cross(0, 1)
+    attend_pair(3)
     wo.serve(2, 2)
-    attend_pair(2)
-    wo.serve(1, 2)
-    wo.cross(0, 1)
     wo.sided(0, False)
     wo.sided(1, False)
-    attend_pair(3)
-    wo.serve(3, 2)
     wo.cross(1, 1)
     attend_pair(4)
+    wo.serve(1, 2)
     wo.cross(2, 1)
+    attend_pair(5)
+    wo.serve(3, 2)
     wo.serve(0, 3)
-    attend_pair(5)
+    attend_pair(6)
     wo.serve(2, 3)
     wo.cross(0, 2)
-    attend_pair(6)
+    wo.cross(3, 1)
+    attend_pair(7)
     wo.serve(1, 3)
-    wo.cross(3, 1)
+    wo.serve(3, 3)
     wo.cross(2, 2)
-    attend_pair(7)
-    wo.serve(3, 3)
     kvw_cross.wait_send()
     for item in (*kvw_lines, wq):
         item.drain()
@@ -625,7 +625,7 @@
 
     def placed_copy(h, k):
         cols = spot_of(h, k)
-        return pltpu.make_async_copy(placed_buf.at[:, cols], out_ref.at[:, cols], placed_sem.at[h, k])
+        return pltpu.make_async_copy(placed_buf.at[:, cols], out_ref.at[:, cols], placed_sem)
 
     def update_wait(h, k):
         remote(out_buf.at[k, 0], update_buf.at[h, k], out_send, out_recv.at[h, k], {"blk": p.across}).wait_recv()
@@ -665,9 +665,7 @@
         meta_copy(0, core).wait_send()
         out_sent(2)
 
-    for k in range(pieces):
-        for h in range(2):
-            placed_copy(h, k).wait()
+    pltpu.make_async_copy(placed_buf, out_ref, placed_sem).wait()
 
 
 def layer(n, keep, hidden, kept_idx, kept_count, router, norm_gain, qk_gain, query_weight, key_weight,
@@ -697,7 +695,7 @@
             dma((len(small),)),
             pltpu.VMEM((cap, width), jnp.bfloat16),
             pltpu.VMEM((tokens, width), jnp.bfloat16),
-            dma((2, pieces)),
+            dma(()),
             pltpu.VMEM((cap, width), jnp.bfloat16),
             pltpu.VMEM((8, cap), jnp.int32),
             pltpu.VMEM((n, 8, cap), jnp.int32),

time: 68.5 us -> 68.1 us (level)
  no operation moved by 1% of the time
where the time goes in v4:
time: 68.1 us; the launch traced here: 68 us
  Pallas kernels  64.1 us (94%)
  local copies, waits for them, and re-layouts  3.16 us (5%)
    pallas_call x1, Pallas kernels, layer(): pl.pallas_call(functools.partial(layer_kernel, n, pieces), out_shape=jax....  64.1 us
    unnamed x1, local copies, waits for them, and re-layouts  3.16 us

profile of v4, /device:TPU:1, one launch (start us, length us, event | category | flops | bytes accessed | tf_op | source)
XLA Modules:
  0.0 68.0 jit_solution(4316752385943748781)
XLA Ops:
  0.7 64.1 %shard_map.109 = bf16[512,2048]{1,0:T(8,128)(2,1)} custom-call(bf16[512,2048]{1,0:T(8,128)(2,1)} %hidden_ref.1, bf16[128,2048]{1,0:T(8,128)(2,1)} %wq_ref.1, bf16[128,2048]{1,0:T(8,128)(2,1)} %wo_ref.1, s32[1,128]{1,0:T(1,128)} %idx_hbm.1, s32[1,1]{1,0:T(1,128)} %bitcast.2.count_hbm, f32[1,2048]{1,0:T(1,128)} %bitcast.3, bf16[2048]{0:T(1024)(128)(2,1)} %router_hbm.1, ...), custom_call_target="tpu_custom_call" | custom-call | tf_op jit(solution)/shard_map/pallas_call | solution.py:688
  64.8 3.2 %copy.14 = bf16[512,2048]{1,0:T(8,128)(2,1)} copy(bf16[512,2048]{1,0:T(8,128)(2,1)} %shard_map.109) | data formatting | bytes 4194304
